TPU v7x, 32 devices: a whole 2x2x4 slice. The times are simulated.
32 devices in a mesh: wide: 16 (over z, y, x), narrow: 2 (over core).
Axes of the slice: x: 2, y: 2, z: 4, core: 2. Of those that a mesh axis runs over, the one named last changes fastest.
Arguments:
- residual_local: float32 [256, 32, 128], P('wide', 'narrow'), may hold values from -6 to 6
- geometry: float32 [3, 256, 32, 128], P(None, 'wide', 'narrow'), may hold values from 0.02 to 0.2
- helmholtz: float32 [256, 32, 128], P('wide', 'narrow'), may hold values from 0.2 to 2
- coarse_ids: int32 [32, 4, 16, 8], P('wide', 'narrow'), may hold values from 1 to 255, as said below
- coarse_correction: float32 [4096], P(('wide', 'narrow')), may hold values from -6 to 6
Outputs:
- preconditioned: float32 [256, 32, 128], P('wide', 'narrow')
- coarse_residual: float32 [4096], P(('wide', 'narrow'))
Inputs may be any that keep to these rules, and one draw needn't show every extreme that they name: `coarse_ids`: within one slab (2 consecutive element planes along the first dimension) the ids number the slab's corner points one to one: corners that elements of the slab share carry the same id, distinct corner points distinct ids. Each slab has its own numbering.
All inputs are finite; a program needn't handle non-finite values.
Results may differ from a plain program's by a relative error of at most 0.0003.
Values sent between devices are 32-bit elements; how exact they have to be, the bound alone decides.
A program may use at most 64 MiB of HBM per device.

v0:
```python
import math

import jax
import jax.numpy as jnp
import numpy as np
from jax import lax
from jax.sharding import PartitionSpec as P

NODES = 8
DEGREE = 3


low_bound = 0.3
high_bound = 3.3
gll_inner = (
    -0.8717401485096066,
    -0.5917001814331423,
    -0.2092992179024789,
    0.2092992179024789,
    0.5917001814331423,
    0.8717401485096066,
)


def with_halo(block, sides, width):
    for axis, dim in sides:
        count = lax.axis_size(axis)
        forward = [(i, i + 1) for i in range(count - 1)]
        backward = [(target, source) for source, target in forward]
        low = lax.ppermute(
            lax.slice_in_dim(block, block.shape[dim] - width, None, axis=dim), axis, forward
        )
        high = lax.ppermute(lax.slice_in_dim(block, 0, width, axis=dim), axis, backward)
        block = jnp.concatenate([low, block, high], axis=dim)
    return block


def legendre_values(points, order):
    previous = points * 0.0 + 1.0
    current = points
    for number in range(1, order):
        previous, current = (
            current,
            ((2 * number + 1) * points * current - number * previous) / (number + 1),
        )
    return current


def tables():
    order = NODES - 1
    points = np.concatenate([np.array([-1.0]), np.array(gll_inner), np.array([1.0])])
    values = legendre_values(points, order)
    eye = np.eye(NODES)
    differ = points[:, None] - points[None, :] + eye
    offdiag = np.where(eye > 0, 0.0, values[:, None] / values[None, :] / differ)
    ends = np.concatenate(
        [
            np.array([-order * (order + 1) / 4.0]),
            np.zeros(NODES - 2),
            np.array([order * (order + 1) / 4.0]),
        ]
    )
    derivative = offdiag + eye * ends[None, :]
    linear = np.stack([(1.0 - points) / 2.0, (1.0 + points) / 2.0], axis=1)
    return (jnp.asarray(derivative, dtype=jnp.float32), jnp.asarray(linear, dtype=jnp.float32))


def element_operator(field, geometry, helmholtz, derivative, block):
    highest = lax.Precision.HIGHEST
    sx, sy, sz = field.shape
    first = field.reshape(sx // NODES, NODES, sy, sz)
    grads = jnp.einsum("ab,ebyz->eayz", derivative, first, precision=highest) * geometry[0].reshape(
        first.shape
    )
    result = jnp.einsum("ab,eayz->ebyz", derivative, grads, precision=highest).reshape(field.shape)
    second = field.reshape(sx, sy // NODES, NODES, sz)
    grads = jnp.einsum("ab,xebz->xeaz", derivative, second, precision=highest) * geometry[
        1
    ].reshape(second.shape)
    result = result + jnp.einsum("ab,xeaz->xebz", derivative, grads, precision=highest).reshape(
        field.shape
    )
    forward = jnp.kron(jnp.eye(block // NODES, dtype=jnp.float32), derivative)
    third = field.reshape(sx, sy, sz // block, block)
    grads = jnp.einsum("xyek,nk->xyen", third, forward, precision=highest) * geometry[2].reshape(
        third.shape
    )
    result = result + jnp.einsum("xyen,nk->xyek", grads, forward, precision=highest).reshape(
        field.shape
    )
    return result + helmholtz * field


def diagonal_part(geometry, helmholtz, derivative, block):
    highest = lax.Precision.HIGHEST
    sx, sy, sz = helmholtz.shape
    square = derivative * derivative
    result = jnp.einsum(
        "ai,eayz->eiyz", square, geometry[0].reshape(sx // NODES, NODES, sy, sz), precision=highest
    ).reshape(helmholtz.shape)
    result = result + jnp.einsum(
        "ai,xeaz->xeiz", square, geometry[1].reshape(sx, sy // NODES, NODES, sz), precision=highest
    ).reshape(helmholtz.shape)
    squares = jnp.kron(jnp.eye(block // NODES, dtype=jnp.float32), square)
    result = result + jnp.einsum(
        "xyen,ni->xyei", geometry[2].reshape(sx, sy, sz // block, block), squares, precision=highest
    ).reshape(helmholtz.shape)
    return result + helmholtz


def face_add(padded, axis, length):
    lower = lax.slice_in_dim(padded, 0, length, axis=axis)
    centre = lax.slice_in_dim(padded, 1, length + 1, axis=axis)
    upper = lax.slice_in_dim(padded, 2, length + 2, axis=axis)
    dims = [1] * padded.ndim
    dims[axis] = length
    places = (jnp.arange(length, dtype=jnp.int32) % NODES).reshape(dims)
    return centre + jnp.where(places == 0, lower, 0.0) + jnp.where(places == NODES - 1, upper, 0.0)


def assemble(field, pieces):
    sx, sy, sz = field.shape
    padded = with_halo(field, (("wide", 0),), 1)
    merged = face_add(padded, 0, sx)
    padded = with_halo(merged, (("narrow", 1),), 1)
    merged = face_add(padded, 1, sy)
    length = sz // pieces
    split = merged.reshape(sx, sy, pieces, length)
    summed = face_add(jnp.pad(split, ((0, 0), (0, 0), (0, 0), (1, 1))), 3, length)
    return summed.reshape(sx, sy, sz)


def inverse_counts(dims_all, starts, totals):
    factors = []
    for axis in range(3):
        length = dims_all[axis]
        places = jnp.arange(length, dtype=jnp.int32)
        spots = starts[axis] + places
        inner = (places % NODES == 0) & (spots > 0) | (places % NODES == NODES - 1) & (
            spots < totals[axis] - 1
        )
        dims = [1, 1, 1]
        dims[axis] = length
        factors.append(jnp.where(inner, 2.0, 1.0).astype(jnp.float32).reshape(dims))
    return 1.0 / (factors[0] * factors[1] * factors[2])


def restrict(field, linear, block):
    highest = lax.Precision.HIGHEST
    sx, sy, sz = field.shape
    expand = jnp.kron(jnp.eye(block // NODES, dtype=jnp.float32), linear)
    along_z = jnp.einsum(
        "xyek,kc->xyec", field.reshape(sx, sy, sz // block, block), expand, precision=highest
    ).reshape(sx, sy, sz // 4)
    along_y = jnp.einsum(
        "jb,xejz->xebz", linear, along_z.reshape(sx, sy // NODES, NODES, sz // 4), precision=highest
    )
    along_x = jnp.einsum(
        "ia,eiybz->eaybz",
        linear,
        along_y.reshape(sx // NODES, NODES, sy // NODES, 2, sz // 4),
        precision=highest,
    )
    cube = along_x.reshape(sx // NODES, 2, sy // NODES, 2, sz // NODES, 2).transpose(
        0, 2, 4, 1, 3, 5
    )
    return cube.reshape(sx // NODES, sy // NODES, sz // NODES, 8)


def prolong(corners, linear, block, sx, sy, sz):
    highest = lax.Precision.HIGHEST
    cube = corners.reshape(sx // NODES, sy // NODES, sz // NODES, 2, 2, 2).transpose(
        0, 3, 1, 4, 2, 5
    )
    cube = cube.reshape(sx // NODES, 2, sy // NODES, 2, sz // 4)
    along_x = jnp.einsum("ia,eaybz->eiybz", linear, cube, precision=highest).reshape(
        sx, sy // NODES, 2, sz // 4
    )
    along_y = jnp.einsum("jb,xebz->xejz", linear, along_x, precision=highest).reshape(
        sx, sy, sz // block, block // 4
    )
    expand = jnp.kron(jnp.eye(block // NODES, dtype=jnp.float32), linear)
    return jnp.einsum("xyec,kc->xyek", along_y, expand, precision=highest).reshape(sx, sy, sz)


def chebyshev(residual, inv_diagonal, apply_operator, count, applies):
    theta = 0.5 * (high_bound + low_bound)
    delta = 0.5 * (high_bound - low_bound)
    sigma = theta / delta
    rho = 1.0 / sigma
    update = inv_diagonal * residual / theta
    solution = jnp.zeros_like(residual)
    for number in range(count):
        solution = solution + update
        if number < applies:
            residual = residual - apply_operator(update)
            if number + 1 < count:
                rho_next = 1.0 / (2.0 * sigma - rho)
                update = rho_next * rho * update + 2.0 * rho_next / delta * inv_diagonal * residual
                rho = rho_next
    return (solution, residual)


def on_device(residual_local, geometry, helmholtz, coarse_ids, coarse_correction):
    derivative, linear = tables()
    sx, sy, sz = residual_local.shape
    block = math.gcd(sz, 128)

    def apply_operator(field):
        return assemble(element_operator(field, geometry, helmholtz, derivative, block), 1)

    whole = lax.all_gather(coarse_correction, "narrow", axis=0, tiled=True)
    correction = prolong(whole[coarse_ids], linear, block, sx, sy, sz)
    local_image = element_operator(correction, geometry, helmholtz, derivative, block)
    stacked = jnp.concatenate(
        [diagonal_part(geometry, helmholtz, derivative, block), residual_local, local_image], axis=2
    )
    assembled = assemble(stacked, 3)
    inv_diagonal = 1.0 / assembled[:, :, :sz]
    rhs = assembled[:, :, sz : 2 * sz]
    correction_image = assembled[:, :, 2 * sz :]
    smoothed, pre_residual = chebyshev(rhs, inv_diagonal, apply_operator, DEGREE, DEGREE)
    starts = (lax.axis_index("wide") * sx, lax.axis_index("narrow") * sy, 0)
    totals = (sx * lax.axis_size("wide"), sy * lax.axis_size("narrow"), sz)
    weights = inverse_counts((sx, sy, sz), starts, totals)
    corners = restrict(pre_residual * weights, linear, block)
    slab_slots = coarse_correction.shape[0] * lax.axis_size("narrow")
    partial_value = jax.ops.segment_sum(
        corners.reshape(-1), coarse_ids.reshape(-1), num_segments=slab_slots
    )
    coarse_residual = lax.psum_scatter(partial_value, "narrow", scatter_dimension=0, tiled=True)
    combined = smoothed + correction
    post_residual = pre_residual - correction_image
    smoothing, unused = chebyshev(post_residual, inv_diagonal, apply_operator, DEGREE, DEGREE - 1)
    return (combined + smoothing, coarse_residual)


def solution(mesh):
    return jax.shard_map(
        on_device,
        mesh=mesh,
        in_specs=(
            P("wide", "narrow", None),
            P(None, "wide", "narrow", None),
            P("wide", "narrow", None),
            P("wide", "narrow", None, None),
            P(("wide", "narrow")),
        ),
        out_specs=(P("wide", "narrow", None), P(("wide", "narrow"))),
        check_vma=False,
    )
```

profile of v0, /device:TPU:0, one launch (start us, length us, event | category | flops | bytes accessed | tf_op | source)
XLA Modules:
  0.0 122.0 jit_solution(1944928360326603104)
XLA Ops:
  3.9 1.9 %all-gather = f32[2,1,128]{2,1,0:T(1,128)S(1)} all-gather(f32[1,1,128]{2,1,0:T(1,128)S(1)} %bitcast.367), channel_id=1, replica_groups=mesh['wide'=16,'narrow'=2] {'narrow'}, dimensions={0}, use_global_device_ids=true | all-gather | bytes 1536 | tf_op jit(solution)/shard_map/all_gather | solution.py:212
  5.9 3.5 %gather_fusion = f32[512]{0:T(512)S(1)} fusion(f32[256]{0:T(256)S(1)} %bitcast.342, s32[1024]{0:T(1024)S(1)} %pad_clamp_fusion), kind=kCustom, calls=%fused_computation | custom fusion | bytes 6144 | tf_op jit(solution)/shard_map/gather | solution.py:213
  17.2 4.7 %collective-permute-start = (f32[1,16,384]{2,1,0:T(8,128)S(1)}, f32[1,16,384]{2,1,0:T(8,128)S(1)}, u32[]{:S(2)}, u32[]{:S(2)}) collective-permute-start(f32[1,16,384]{2,1,0:T(8,128)S(1)} %get-tuple-element.12), channel_id=1, source_target_pairs={{0,2},{2,4},{4,6},{6,8},{8,10},{10,12},{12,14},{14,16},{16,18},{18... | collective-permute-start | bytes 73736 | tf_op jit(solution)/shard_map/ppermute | solution.py:30
  22.0 1.3 %collective-permute-start.1 = (f32[1,16,384]{2,1,0:T(8,128)S(1)}, f32[1,16,384]{2,1,0:T(8,128)S(1)}, u32[]{:S(2)}, u32[]{:S(2)}) collective-permute-start(f32[1,16,384]{2,1,0:T(8,128)S(1)} %get-tuple-element.13), channel_id=1, source_target_pairs={{2,0},{4,2},{6,4},{8,6},{10,8},{12,10},{14,12},{16,14},{18,16},{20... | collective-permute-start | bytes 73736 | tf_op jit(solution)/shard_map/ppermute | solution.py:33
  23.5 4.2 %collective-permute-done.1 = f32[1,16,384]{2,1,0:T(8,128)S(1)} collective-permute-done((f32[1,16,384]{2,1,0:T(8,128)S(1)}, f32[1,16,384]{2,1,0:T(8,128)S(1)}, u32[]{:S(2)}, u32[]{:S(2)}) %collective-permute-start.1) | collective-permute-done | bytes 24608 | tf_op jit(solution)/shard_map/ppermute | solution.py:33
  29.2 1.3 %collective-permute-start.3 = (f32[16,1,384]{2,1,0:T(1,128)S(1)}, f32[16,1,384]{2,1,0:T(1,128)S(1)}, u32[]{:S(2)}, u32[]{:S(2)}) collective-permute-start(f32[16,1,384]{2,1,0:T(1,128)S(1)} %get-tuple-element.11), channel_id=1, source_target_pairs={{1,0},{3,2},{5,4},{7,6},{9,8},{11,10},{13,12},{15,14},{17,16},{19,... | collective-permute-start | bytes 73736 | tf_op jit(solution)/shard_map/ppermute | solution.py:33
  30.5 1.8 %collective-permute-done.3 = f32[16,1,384]{2,1,0:T(1,128)S(1)} collective-permute-done((f32[16,1,384]{2,1,0:T(1,128)S(1)}, f32[16,1,384]{2,1,0:T(1,128)S(1)}, u32[]{:S(2)}, u32[]{:S(2)}) %collective-permute-start.3) | collective-permute-done | bytes 24608 | tf_op jit(solution)/shard_map/ppermute | solution.py:33
  35.3 4.3 %collective-permute-start.4 = (f32[1,16,128]{2,1,0:T(8,128)S(1)}, f32[1,16,128]{2,1,0:T(8,128)S(1)}, u32[]{:S(2)}, u32[]{:S(2)}) collective-permute-start(f32[1,16,128]{2,1,0:T(8,128)S(1)} %get-tuple-element.32), channel_id=1, source_target_pairs={{0,2},{2,4},{4,6},{6,8},{8,10},{10,12},{12,14},{14,16},{16,18},{18... | collective-permute-start | bytes 24584 | tf_op jit(solution)/shard_map/ppermute | solution.py:30
  39.6 1.3 %collective-permute-start.5 = (f32[1,16,128]{2,1,0:T(8,128)S(1)}, f32[1,16,128]{2,1,0:T(8,128)S(1)}, u32[]{:S(2)}, u32[]{:S(2)}) collective-permute-start(f32[1,16,128]{2,1,0:T(8,128)S(1)} %get-tuple-element.33), channel_id=1, source_target_pairs={{2,0},{4,2},{6,4},{8,6},{10,8},{12,10},{14,12},{16,14},{18,16},{20... | collective-permute-start | bytes 24584 | tf_op jit(solution)/shard_map/ppermute | solution.py:33
  40.9 4.2 %collective-permute-done.5 = f32[1,16,128]{2,1,0:T(8,128)S(1)} collective-permute-done((f32[1,16,128]{2,1,0:T(8,128)S(1)}, f32[1,16,128]{2,1,0:T(8,128)S(1)}, u32[]{:S(2)}, u32[]{:S(2)}) %collective-permute-start.5) | collective-permute-done | bytes 8224 | tf_op jit(solution)/shard_map/ppermute | solution.py:33
  46.6 1.3 %collective-permute-start.7 = (f32[16,1,128]{2,1,0:T(1,128)S(1)}, f32[16,1,128]{2,1,0:T(1,128)S(1)}, u32[]{:S(2)}, u32[]{:S(2)}) collective-permute-start(f32[16,1,128]{2,1,0:T(1,128)S(1)} %get-tuple-element.31), channel_id=1, source_target_pairs={{1,0},{3,2},{5,4},{7,6},{9,8},{11,10},{13,12},{15,14},{17,16},{19,... | collective-permute-start | bytes 24584 | tf_op jit(solution)/shard_map/ppermute | solution.py:33
  47.9 1.8 %collective-permute-done.7 = f32[16,1,128]{2,1,0:T(1,128)S(1)} collective-permute-done((f32[16,1,128]{2,1,0:T(1,128)S(1)}, f32[16,1,128]{2,1,0:T(1,128)S(1)}, u32[]{:S(2)}, u32[]{:S(2)}) %collective-permute-start.7) | collective-permute-done | bytes 8224 | tf_op jit(solution)/shard_map/ppermute | solution.py:33
  51.6 3.8 %collective-permute-start.8 = (f32[1,16,128]{2,1,0:T(8,128)S(1)}, f32[1,16,128]{2,1,0:T(8,128)S(1)}, u32[]{:S(2)}, u32[]{:S(2)}) collective-permute-start(f32[1,16,128]{2,1,0:T(8,128)S(1)} %get-tuple-element.28), channel_id=1, source_target_pairs={{0,2},{2,4},{4,6},{6,8},{8,10},{10,12},{12,14},{14,16},{16,18},{18... | collective-permute-start | bytes 24584 | tf_op jit(solution)/shard_map/ppermute | solution.py:30
  55.4 1.3 %collective-permute-start.9 = (f32[1,16,128]{2,1,0:T(8,128)S(1)}, f32[1,16,128]{2,1,0:T(8,128)S(1)}, u32[]{:S(2)}, u32[]{:S(2)}) collective-permute-start(f32[1,16,128]{2,1,0:T(8,128)S(1)} %get-tuple-element.29), channel_id=1, source_target_pairs={{2,0},{4,2},{6,4},{8,6},{10,8},{12,10},{14,12},{16,14},{18,16},{20... | collective-permute-start | bytes 24584 | tf_op jit(solution)/shard_map/ppermute | solution.py:33
  56.8 4.2 %collective-permute-done.9 = f32[1,16,128]{2,1,0:T(8,128)S(1)} collective-permute-done((f32[1,16,128]{2,1,0:T(8,128)S(1)}, f32[1,16,128]{2,1,0:T(8,128)S(1)}, u32[]{:S(2)}, u32[]{:S(2)}) %collective-permute-start.9) | collective-permute-done | bytes 8224 | tf_op jit(solution)/shard_map/ppermute | solution.py:33
  62.4 1.3 %collective-permute-start.11 = (f32[16,1,128]{2,1,0:T(1,128)S(1)}, f32[16,1,128]{2,1,0:T(1,128)S(1)}, u32[]{:S(2)}, u32[]{:S(2)}) collective-permute-start(f32[16,1,128]{2,1,0:T(1,128)S(1)} %get-tuple-element.27), channel_id=1, source_target_pairs={{1,0},{3,2},{5,4},{7,6},{9,8},{11,10},{13,12},{15,14},{17,16},{19,... | collective-permute-start | bytes 24584 | tf_op jit(solution)/shard_map/ppermute | solution.py:33
  63.7 1.7 %collective-permute-done.11 = f32[16,1,128]{2,1,0:T(1,128)S(1)} collective-permute-done((f32[16,1,128]{2,1,0:T(1,128)S(1)}, f32[16,1,128]{2,1,0:T(1,128)S(1)}, u32[]{:S(2)}, u32[]{:S(2)}) %collective-permute-start.11) | collective-permute-done | bytes 8224 | tf_op jit(solution)/shard_map/ppermute | solution.py:33
  67.5 4.8 %collective-permute-start.12 = (f32[1,16,128]{2,1,0:T(8,128)S(1)}, f32[1,16,128]{2,1,0:T(8,128)S(1)}, u32[]{:S(2)}, u32[]{:S(2)}) collective-permute-start(f32[1,16,128]{2,1,0:T(8,128)S(1)} %get-tuple-element.24), channel_id=1, source_target_pairs={{0,2},{2,4},{4,6},{6,8},{8,10},{10,12},{12,14},{14,16},{16,18},{18... | collective-permute-start | bytes 24584 | tf_op jit(solution)/shard_map/ppermute | solution.py:30
  72.3 1.3 %collective-permute-start.13 = (f32[1,16,128]{2,1,0:T(8,128)S(1)}, f32[1,16,128]{2,1,0:T(8,128)S(1)}, u32[]{:S(2)}, u32[]{:S(2)}) collective-permute-start(f32[1,16,128]{2,1,0:T(8,128)S(1)} %get-tuple-element.25), channel_id=1, source_target_pairs={{2,0},{4,2},{6,4},{8,6},{10,8},{12,10},{14,12},{16,14},{18,16},{20... | collective-permute-start | bytes 24584 | tf_op jit(solution)/shard_map/ppermute | solution.py:33
  73.7 4.2 %collective-permute-done.13 = f32[1,16,128]{2,1,0:T(8,128)S(1)} collective-permute-done((f32[1,16,128]{2,1,0:T(8,128)S(1)}, f32[1,16,128]{2,1,0:T(8,128)S(1)}, u32[]{:S(2)}, u32[]{:S(2)}) %collective-permute-start.13) | collective-permute-done | bytes 8224 | tf_op jit(solution)/shard_map/ppermute | solution.py:33
  79.3 1.3 %collective-permute-start.15 = (f32[16,1,128]{2,1,0:T(1,128)S(1)}, f32[16,1,128]{2,1,0:T(1,128)S(1)}, u32[]{:S(2)}, u32[]{:S(2)}) collective-permute-start(f32[16,1,128]{2,1,0:T(1,128)S(1)} %get-tuple-element.23), channel_id=1, source_target_pairs={{1,0},{3,2},{5,4},{7,6},{9,8},{11,10},{13,12},{15,14},{17,16},{19,... | collective-permute-start | bytes 24584 | tf_op jit(solution)/shard_map/ppermute | solution.py:33
  80.7 1.7 %collective-permute-done.15 = f32[16,1,128]{2,1,0:T(1,128)S(1)} collective-permute-done((f32[16,1,128]{2,1,0:T(1,128)S(1)}, f32[16,1,128]{2,1,0:T(1,128)S(1)}, u32[]{:S(2)}, u32[]{:S(2)}) %collective-permute-start.15) | collective-permute-done | bytes 8224 | tf_op jit(solution)/shard_map/ppermute | solution.py:33
  84.4 3.7 %collective-permute-start.16 = (f32[1,16,128]{2,1,0:T(8,128)S(1)}, f32[1,16,128]{2,1,0:T(8,128)S(1)}, u32[]{:S(2)}, u32[]{:S(2)}) collective-permute-start(f32[1,16,128]{2,1,0:T(8,128)S(1)} %get-tuple-element.20), channel_id=1, source_target_pairs={{0,2},{2,4},{4,6},{6,8},{8,10},{10,12},{12,14},{14,16},{16,18},{18... | collective-permute-start | bytes 24584 | tf_op jit(solution)/shard_map/ppermute | solution.py:30
  88.1 1.5 %collective-permute-start.17 = (f32[1,16,128]{2,1,0:T(8,128)S(1)}, f32[1,16,128]{2,1,0:T(8,128)S(1)}, u32[]{:S(2)}, u32[]{:S(2)}) collective-permute-start(f32[1,16,128]{2,1,0:T(8,128)S(1)} %get-tuple-element.21), channel_id=1, source_target_pairs={{2,0},{4,2},{6,4},{8,6},{10,8},{12,10},{14,12},{16,14},{18,16},{20... | collective-permute-start | bytes 24584 | tf_op jit(solution)/shard_map/ppermute | solution.py:33
  91.9 2.0 %collective-permute-done.17 = f32[1,16,128]{2,1,0:T(8,128)S(1)} collective-permute-done((f32[1,16,128]{2,1,0:T(8,128)S(1)}, f32[1,16,128]{2,1,0:T(8,128)S(1)}, u32[]{:S(2)}, u32[]{:S(2)}) %collective-permute-start.17) | collective-permute-done | bytes 8224 | tf_op jit(solution)/shard_map/ppermute | solution.py:33
  95.3 1.3 %collective-permute-start.19 = (f32[16,1,128]{2,1,0:T(1,128)S(1)}, f32[16,1,128]{2,1,0:T(1,128)S(1)}, u32[]{:S(2)}, u32[]{:S(2)}) collective-permute-start(f32[16,1,128]{2,1,0:T(1,128)S(1)} %get-tuple-element.19), channel_id=1, source_target_pairs={{1,0},{3,2},{5,4},{7,6},{9,8},{11,10},{13,12},{15,14},{17,16},{19,... | collective-permute-start | bytes 24584 | tf_op jit(solution)/shard_map/ppermute | solution.py:33
  96.9 1.4 %collective-permute-done.19 = f32[16,1,128]{2,1,0:T(1,128)S(1)} collective-permute-done((f32[16,1,128]{2,1,0:T(1,128)S(1)}, f32[16,1,128]{2,1,0:T(1,128)S(1)}, u32[]{:S(2)}, u32[]{:S(2)}) %collective-permute-start.19) | collective-permute-done | bytes 8224 | tf_op jit(solution)/shard_map/ppermute | solution.py:33
  100.4 4.0 %collective-permute-start.20 = (f32[1,16,128]{2,1,0:T(8,128)S(1)}, f32[1,16,128]{2,1,0:T(8,128)S(1)}, u32[]{:S(2)}, u32[]{:S(2)}) collective-permute-start(f32[1,16,128]{2,1,0:T(8,128)S(1)} %get-tuple-element.16), channel_id=1, source_target_pairs={{0,2},{2,4},{4,6},{6,8},{8,10},{10,12},{12,14},{14,16},{16,18},{18... | collective-permute-start | bytes 24584 | tf_op jit(solution)/shard_map/ppermute | solution.py:30
  104.4 1.3 %collective-permute-start.21 = (f32[1,16,128]{2,1,0:T(8,128)S(1)}, f32[1,16,128]{2,1,0:T(8,128)S(1)}, u32[]{:S(2)}, u32[]{:S(2)}) collective-permute-start(f32[1,16,128]{2,1,0:T(8,128)S(1)} %get-tuple-element.17), channel_id=1, source_target_pairs={{2,0},{4,2},{6,4},{8,6},{10,8},{12,10},{14,12},{16,14},{18,16},{20... | collective-permute-start | bytes 24584 | tf_op jit(solution)/shard_map/ppermute | solution.py:33
  105.9 4.0 %collective-permute-done.21 = f32[1,16,128]{2,1,0:T(8,128)S(1)} collective-permute-done((f32[1,16,128]{2,1,0:T(8,128)S(1)}, f32[1,16,128]{2,1,0:T(8,128)S(1)}, u32[]{:S(2)}, u32[]{:S(2)}) %collective-permute-start.21) | collective-permute-done | bytes 8224 | tf_op jit(solution)/shard_map/ppermute | solution.py:33
  113.2 4.1 %scatter_custom_fusion = f32[256]{0:T(256)S(1)} fusion(s32[512]{0:T(512)S(1)} %reshape.473, f32[512]{0:T(512)S(1)} %reshape.475, f32[]{:T(128)} %constant.141.clone.1), kind=kCustom, calls=%fused_computation.253 | custom fusion | flops 512 | bytes 1028 | tf_op jit(solution)/shard_map/scatter-add | solution.py:228
  117.3 3.3 %all-reduce.6 = f32[256]{0:T(256)S(1)} all-reduce(f32[256]{0:T(256)S(1)} %scatter_custom_fusion), channel_id=2, replica_groups=mesh['wide'=16,'narrow'=2] {'narrow'}, use_global_device_ids=true, to_apply=%region_1.2.clone | all-reduce | flops 256 | bytes 2048
  (162 shorter events, 35.9 us)
Async XLA Ops:
  0.6 0.7 copy-start.6
  0.7 0.7 copy-start.7
  2.3 0.7 copy-start.4
  9.4 1.2 copy-start
  11.8 0.7 copy-start.2
  13.4 0.7 copy-start.5
  15.1 0.9 copy-start.1
  16.3 0.9 copy-start.3
  17.2 6.2 %collective-permute-start = (f32[1,16,384]{2,1,0:T(8,128)S(1)}, f32[1,16,384]{2,1,0:T(8,128)S(1)}, u32[]{:S(2)}, u32[]{:S(2)}) collective-permute-start(f32[1,16,384]{2,1,0:T(8,128)S(1)} %get-tuple-element.12), channel_id=1, source_target_pairs={{0,2},{2,4},{4,6},{6,8},{8,10},{10,12},{12,14},{14,16},{16,18},{18... | collective-permute-start | bytes 73736 | tf_op jit(solution)/shard_map/ppermute | solution.py:30
  22.0 5.7 %collective-permute-start.1 = (f32[1,16,384]{2,1,0:T(8,128)S(1)}, f32[1,16,384]{2,1,0:T(8,128)S(1)}, u32[]{:S(2)}, u32[]{:S(2)}) collective-permute-start(f32[1,16,384]{2,1,0:T(8,128)S(1)} %get-tuple-element.13), channel_id=1, source_target_pairs={{2,0},{4,2},{6,4},{8,6},{10,8},{12,10},{14,12},{16,14},{18,16},{20... | collective-permute-start | bytes 73736 | tf_op jit(solution)/shard_map/ppermute | solution.py:33
  27.9 2.6 %collective-permute-start.2 = (f32[16,1,384]{2,1,0:T(1,128)S(1)}, f32[16,1,384]{2,1,0:T(1,128)S(1)}, u32[]{:S(2)}, u32[]{:S(2)}) collective-permute-start(f32[16,1,384]{2,1,0:T(1,128)S(1)} %get-tuple-element.10), channel_id=1, source_target_pairs={{0,1},{2,3},{4,5},{6,7},{8,9},{10,11},{12,13},{14,15},{16,17},{18,... | collective-permute-start | bytes 73736 | tf_op jit(solution)/shard_map/ppermute | solution.py:30
  29.2 3.1 %collective-permute-start.3 = (f32[16,1,384]{2,1,0:T(1,128)S(1)}, f32[16,1,384]{2,1,0:T(1,128)S(1)}, u32[]{:S(2)}, u32[]{:S(2)}) collective-permute-start(f32[16,1,384]{2,1,0:T(1,128)S(1)} %get-tuple-element.11), channel_id=1, source_target_pairs={{1,0},{3,2},{5,4},{7,6},{9,8},{11,10},{13,12},{15,14},{17,16},{19,... | collective-permute-start | bytes 73736 | tf_op jit(solution)/shard_map/ppermute | solution.py:33
  35.3 5.6 %collective-permute-start.4 = (f32[1,16,128]{2,1,0:T(8,128)S(1)}, f32[1,16,128]{2,1,0:T(8,128)S(1)}, u32[]{:S(2)}, u32[]{:S(2)}) collective-permute-start(f32[1,16,128]{2,1,0:T(8,128)S(1)} %get-tuple-element.32), channel_id=1, source_target_pairs={{0,2},{2,4},{4,6},{6,8},{8,10},{10,12},{12,14},{14,16},{16,18},{18... | collective-permute-start | bytes 24584 | tf_op jit(solution)/shard_map/ppermute | solution.py:30
  39.6 5.5 %collective-permute-start.5 = (f32[1,16,128]{2,1,0:T(8,128)S(1)}, f32[1,16,128]{2,1,0:T(8,128)S(1)}, u32[]{:S(2)}, u32[]{:S(2)}) collective-permute-start(f32[1,16,128]{2,1,0:T(8,128)S(1)} %get-tuple-element.33), channel_id=1, source_target_pairs={{2,0},{4,2},{6,4},{8,6},{10,8},{12,10},{14,12},{16,14},{18,16},{20... | collective-permute-start | bytes 24584 | tf_op jit(solution)/shard_map/ppermute | solution.py:33
  45.3 2.6 %collective-permute-start.6 = (f32[16,1,128]{2,1,0:T(1,128)S(1)}, f32[16,1,128]{2,1,0:T(1,128)S(1)}, u32[]{:S(2)}, u32[]{:S(2)}) collective-permute-start(f32[16,1,128]{2,1,0:T(1,128)S(1)} %get-tuple-element.30), channel_id=1, source_target_pairs={{0,1},{2,3},{4,5},{6,7},{8,9},{10,11},{12,13},{14,15},{16,17},{18,... | collective-permute-start | bytes 24584 | tf_op jit(solution)/shard_map/ppermute | solution.py:30
  46.6 3.1 %collective-permute-start.7 = (f32[16,1,128]{2,1,0:T(1,128)S(1)}, f32[16,1,128]{2,1,0:T(1,128)S(1)}, u32[]{:S(2)}, u32[]{:S(2)}) collective-permute-start(f32[16,1,128]{2,1,0:T(1,128)S(1)} %get-tuple-element.31), channel_id=1, source_target_pairs={{1,0},{3,2},{5,4},{7,6},{9,8},{11,10},{13,12},{15,14},{17,16},{19,... | collective-permute-start | bytes 24584 | tf_op jit(solution)/shard_map/ppermute | solution.py:33
  51.6 5.1 %collective-permute-start.8 = (f32[1,16,128]{2,1,0:T(8,128)S(1)}, f32[1,16,128]{2,1,0:T(8,128)S(1)}, u32[]{:S(2)}, u32[]{:S(2)}) collective-permute-start(f32[1,16,128]{2,1,0:T(8,128)S(1)} %get-tuple-element.28), channel_id=1, source_target_pairs={{0,2},{2,4},{4,6},{6,8},{8,10},{10,12},{12,14},{14,16},{16,18},{18... | collective-permute-start | bytes 24584 | tf_op jit(solution)/shard_map/ppermute | solution.py:30
  55.4 5.5 %collective-permute-start.9 = (f32[1,16,128]{2,1,0:T(8,128)S(1)}, f32[1,16,128]{2,1,0:T(8,128)S(1)}, u32[]{:S(2)}, u32[]{:S(2)}) collective-permute-start(f32[1,16,128]{2,1,0:T(8,128)S(1)} %get-tuple-element.29), channel_id=1, source_target_pairs={{2,0},{4,2},{6,4},{8,6},{10,8},{12,10},{14,12},{16,14},{18,16},{20... | collective-permute-start | bytes 24584 | tf_op jit(solution)/shard_map/ppermute | solution.py:33
  61.1 2.6 %collective-permute-start.10 = (f32[16,1,128]{2,1,0:T(1,128)S(1)}, f32[16,1,128]{2,1,0:T(1,128)S(1)}, u32[]{:S(2)}, u32[]{:S(2)}) collective-permute-start(f32[16,1,128]{2,1,0:T(1,128)S(1)} %get-tuple-element.26), channel_id=1, source_target_pairs={{0,1},{2,3},{4,5},{6,7},{8,9},{10,11},{12,13},{14,15},{16,17},{18,... | collective-permute-start | bytes 24584 | tf_op jit(solution)/shard_map/ppermute | solution.py:30
  62.4 3.1 %collective-permute-start.11 = (f32[16,1,128]{2,1,0:T(1,128)S(1)}, f32[16,1,128]{2,1,0:T(1,128)S(1)}, u32[]{:S(2)}, u32[]{:S(2)}) collective-permute-start(f32[16,1,128]{2,1,0:T(1,128)S(1)} %get-tuple-element.27), channel_id=1, source_target_pairs={{1,0},{3,2},{5,4},{7,6},{9,8},{11,10},{13,12},{15,14},{17,16},{19,... | collective-permute-start | bytes 24584 | tf_op jit(solution)/shard_map/ppermute | solution.py:33
  67.5 6.2 %collective-permute-start.12 = (f32[1,16,128]{2,1,0:T(8,128)S(1)}, f32[1,16,128]{2,1,0:T(8,128)S(1)}, u32[]{:S(2)}, u32[]{:S(2)}) collective-permute-start(f32[1,16,128]{2,1,0:T(8,128)S(1)} %get-tuple-element.24), channel_id=1, source_target_pairs={{0,2},{2,4},{4,6},{6,8},{8,10},{10,12},{12,14},{14,16},{16,18},{18... | collective-permute-start | bytes 24584 | tf_op jit(solution)/shard_map/ppermute | solution.py:30
  72.3 5.5 %collective-permute-start.13 = (f32[1,16,128]{2,1,0:T(8,128)S(1)}, f32[1,16,128]{2,1,0:T(8,128)S(1)}, u32[]{:S(2)}, u32[]{:S(2)}) collective-permute-start(f32[1,16,128]{2,1,0:T(8,128)S(1)} %get-tuple-element.25), channel_id=1, source_target_pairs={{2,0},{4,2},{6,4},{8,6},{10,8},{12,10},{14,12},{16,14},{18,16},{20... | collective-permute-start | bytes 24584 | tf_op jit(solution)/shard_map/ppermute | solution.py:33
  78.0 2.7 %collective-permute-start.14 = (f32[16,1,128]{2,1,0:T(1,128)S(1)}, f32[16,1,128]{2,1,0:T(1,128)S(1)}, u32[]{:S(2)}, u32[]{:S(2)}) collective-permute-start(f32[16,1,128]{2,1,0:T(1,128)S(1)} %get-tuple-element.22), channel_id=1, source_target_pairs={{0,1},{2,3},{4,5},{6,7},{8,9},{10,11},{12,13},{14,15},{16,17},{18,... | collective-permute-start | bytes 24584 | tf_op jit(solution)/shard_map/ppermute | solution.py:30
  79.3 3.1 %collective-permute-start.15 = (f32[16,1,128]{2,1,0:T(1,128)S(1)}, f32[16,1,128]{2,1,0:T(1,128)S(1)}, u32[]{:S(2)}, u32[]{:S(2)}) collective-permute-start(f32[16,1,128]{2,1,0:T(1,128)S(1)} %get-tuple-element.23), channel_id=1, source_target_pairs={{1,0},{3,2},{5,4},{7,6},{9,8},{11,10},{13,12},{15,14},{17,16},{19,... | collective-permute-start | bytes 24584 | tf_op jit(solution)/shard_map/ppermute | solution.py:33
  84.4 7.4 %collective-permute-start.16 = (f32[1,16,128]{2,1,0:T(8,128)S(1)}, f32[1,16,128]{2,1,0:T(8,128)S(1)}, u32[]{:S(2)}, u32[]{:S(2)}) collective-permute-start(f32[1,16,128]{2,1,0:T(8,128)S(1)} %get-tuple-element.20), channel_id=1, source_target_pairs={{0,2},{2,4},{4,6},{6,8},{8,10},{10,12},{12,14},{14,16},{16,18},{18... | collective-permute-start | bytes 24584 | tf_op jit(solution)/shard_map/ppermute | solution.py:30
  88.1 5.7 %collective-permute-start.17 = (f32[1,16,128]{2,1,0:T(8,128)S(1)}, f32[1,16,128]{2,1,0:T(8,128)S(1)}, u32[]{:S(2)}, u32[]{:S(2)}) collective-permute-start(f32[1,16,128]{2,1,0:T(8,128)S(1)} %get-tuple-element.21), channel_id=1, source_target_pairs={{2,0},{4,2},{6,4},{8,6},{10,8},{12,10},{14,12},{16,14},{18,16},{20... | collective-permute-start | bytes 24584 | tf_op jit(solution)/shard_map/ppermute | solution.py:33
  94.0 2.9 %collective-permute-start.18 = (f32[16,1,128]{2,1,0:T(1,128)S(1)}, f32[16,1,128]{2,1,0:T(1,128)S(1)}, u32[]{:S(2)}, u32[]{:S(2)}) collective-permute-start(f32[16,1,128]{2,1,0:T(1,128)S(1)} %get-tuple-element.18), channel_id=1, source_target_pairs={{0,1},{2,3},{4,5},{6,7},{8,9},{10,11},{12,13},{14,15},{16,17},{18,... | collective-permute-start | bytes 24584 | tf_op jit(solution)/shard_map/ppermute | solution.py:30
  95.3 3.1 %collective-permute-start.19 = (f32[16,1,128]{2,1,0:T(1,128)S(1)}, f32[16,1,128]{2,1,0:T(1,128)S(1)}, u32[]{:S(2)}, u32[]{:S(2)}) collective-permute-start(f32[16,1,128]{2,1,0:T(1,128)S(1)} %get-tuple-element.19), channel_id=1, source_target_pairs={{1,0},{3,2},{5,4},{7,6},{9,8},{11,10},{13,12},{15,14},{17,16},{19,... | collective-permute-start | bytes 24584 | tf_op jit(solution)/shard_map/ppermute | solution.py:33
  100.4 5.5 %collective-permute-start.20 = (f32[1,16,128]{2,1,0:T(8,128)S(1)}, f32[1,16,128]{2,1,0:T(8,128)S(1)}, u32[]{:S(2)}, u32[]{:S(2)}) collective-permute-start(f32[1,16,128]{2,1,0:T(8,128)S(1)} %get-tuple-element.16), channel_id=1, source_target_pairs={{0,2},{2,4},{4,6},{6,8},{8,10},{10,12},{12,14},{14,16},{16,18},{18... | collective-permute-start | bytes 24584 | tf_op jit(solution)/shard_map/ppermute | solution.py:30
  104.4 5.5 %collective-permute-start.21 = (f32[1,16,128]{2,1,0:T(8,128)S(1)}, f32[1,16,128]{2,1,0:T(8,128)S(1)}, u32[]{:S(2)}, u32[]{:S(2)}) collective-permute-start(f32[1,16,128]{2,1,0:T(8,128)S(1)} %get-tuple-element.17), channel_id=1, source_target_pairs={{2,0},{4,2},{6,4},{8,6},{10,8},{12,10},{14,12},{16,14},{18,16},{20... | collective-permute-start | bytes 24584 | tf_op jit(solution)/shard_map/ppermute | solution.py:33
  110.1 11.1 %collective-permute-start.22 = (f32[16,1,128]{2,1,0:T(1,128)S(1)}, f32[16,1,128]{2,1,0:T(1,128)S(1)}, u32[]{:S(2)}, u32[]{:S(2)}) collective-permute-start(f32[16,1,128]{2,1,0:T(1,128)S(1)} %get-tuple-element.14), channel_id=1, source_target_pairs={{0,1},{2,3},{4,5},{6,7},{8,9},{10,11},{12,13},{14,15},{16,17},{18,... | collective-permute-start | bytes 24584 | tf_op jit(solution)/shard_map/ppermute | solution.py:30
  111.4 9.8 %collective-permute-start.23 = (f32[16,1,128]{2,1,0:T(1,128)S(1)}, f32[16,1,128]{2,1,0:T(1,128)S(1)}, u32[]{:S(2)}, u32[]{:S(2)}) collective-permute-start(f32[16,1,128]{2,1,0:T(1,128)S(1)} %get-tuple-element.15), channel_id=1, source_target_pairs={{1,0},{3,2},{5,4},{7,6},{9,8},{11,10},{13,12},{15,14},{17,16},{19,... | collective-permute-start | bytes 24584 | tf_op jit(solution)/shard_map/ppermute | solution.py:33
  (5 other events, 3.4 us)
where the time goes:
time: 124 us; the launch traced here: 122 us
  starting transfers between devices  48.8 us (39%)
  waiting for transfers between devices  31.5 us (25%)
  local copies, waits for them, and re-layouts  13.9 us (11%)
  matrix products  12.4 us (10%)
  other arithmetic  7.79 us (6%)
  blocking collectives  5.2 us (4%)
  between operations  2.41 us (2%)
    ppermute x12, starting transfers between devices, with_halo(): lax.ppermute(lax.slice_in_dim(block, block.shape[dim] - width, None, axis...  33.1 us
    ppermute x12, waiting for transfers between devices, with_halo(): lax.ppermute(lax.slice_in_dim(block, 0, width, axis=dim), axis, backward)  31.2 us
    ppermute x12, starting transfers between devices, with_halo(): lax.ppermute(lax.slice_in_dim(block, 0, width, axis=dim), axis, backward)  15.7 us
    unnamed x29, local copies, waits for them, and re-layouts  7.38 us
    scatter-add x1, other arithmetic, on_device(): jax.ops.segment_sum(corners.reshape(-1), coarse_ids.reshape(-1), num_segm...  4.09 us
    gather x1, local copies, waits for them, and re-layouts, on_device(): correction = prolong(whole[coarse_ids], linear, block, sx, sy, sz)  3.5 us
    unnamed x1, blocking collectives  3.26 us
  transfers between devices with their start and end apart: 24, of which 12 were waited for; matrix products, arithmetic and copies ran while one was open for 6% of the time, Pallas kernels for 0%

commit v1 on v0

v1 whole, which is shorter than its diff:
```python
import functools
import math

import jax
import jax.numpy as jnp
import numpy as np
from jax import lax
from jax.experimental import pallas as pl
from jax.experimental.pallas import tpu as pltpu
from jax.sharding import PartitionSpec as P

NODES = 8
DEGREE = 3
MESH = pl.DeviceIdType.MESH
HIGHEST = lax.Precision.HIGHEST

low_bound = 0.3
high_bound = 3.3
gll_inner = (
    -0.8717401485096066,
    -0.5917001814331423,
    -0.2092992179024789,
    0.2092992179024789,
    0.5917001814331423,
    0.8717401485096066,
)

DIRS = ((-1, 0), (1, 0), (-1, -1), (-1, 1), (1, -1), (1, 1), (0, -1), (0, 1))
OPPOSITE = tuple(DIRS.index((-a, -b)) for a, b in DIRS)

DIAG, RES, CORR, FIRST = 0, 1, 2, 3
FIELDS = FIRST + 2 * DEGREE - 1


def legendre_values(points, order):
    previous = points * 0.0 + 1.0
    current = points
    for number in range(1, order):
        previous, current = (
            current,
            ((2 * number + 1) * points * current - number * previous) / (number + 1),
        )
    return current


def tables():
    order = NODES - 1
    points = np.concatenate([np.array([-1.0]), np.array(gll_inner), np.array([1.0])])
    values = legendre_values(points, order)
    eye = np.eye(NODES)
    differ = points[:, None] - points[None, :] + eye
    offdiag = np.where(eye > 0, 0.0, values[:, None] / values[None, :] / differ)
    ends = np.concatenate(
        [
            np.array([-order * (order + 1) / 4.0]),
            np.zeros(NODES - 2),
            np.array([order * (order + 1) / 4.0]),
        ]
    )
    derivative = offdiag + eye * ends[None, :]
    linear = np.stack([(1.0 - points) / 2.0, (1.0 + points) / 2.0], axis=1)
    return derivative.astype(np.float32), linear.astype(np.float32)


def halves(matrix):
    matrix = matrix.astype(np.float32)
    high = matrix.astype(jnp.bfloat16)
    low = (matrix - high.astype(np.float32)).astype(jnp.bfloat16)
    return high, low


def left_table(matrix):
    return np.stack(halves(matrix))


def right_table(matrix):
    high, low = halves(matrix)
    return np.block([[high, low], [high, np.zeros_like(low)]])


def split(value):
    high = value.astype(jnp.bfloat16)
    low = (value - high.astype(jnp.float32)).astype(jnp.bfloat16)
    return high, low


def dot(a, b):
    return jnp.dot(a, b, preferred_element_type=jnp.float32)


def left(table, value):
    high, low = split(value)
    n = value.shape[1]
    both = dot(table[0], jnp.concatenate([high, low], axis=1))
    return both[:, :n] + both[:, n:] + dot(table[1], high)


def right(value, table):
    high, low = split(value)
    n = value.shape[1]
    both = dot(jnp.concatenate([high, low], axis=1), table[...])
    return both[:, :n] + both[:, n:]


def three_rows(row):
    high = row.astype(jnp.bfloat16).astype(jnp.float32)
    rest = row - high
    mid = rest.astype(jnp.bfloat16).astype(jnp.float32)
    low = rest - mid
    place = lax.broadcasted_iota(jnp.int32, (8, row.shape[1]), 0)
    zero = jnp.zeros((8, row.shape[1]), jnp.float32)
    return jnp.where(
        place == 0, high, jnp.where(place == 1, mid, jnp.where(place == 2, low, zero))
    ).astype(jnp.bfloat16)


def kernel(
    sizes,
    derivative,
    res_ref,
    geo_ref,
    hel_ref,
    ids_ref,
    cc_ref,
    dy_ref,
    dyt_ref,
    sqy_ref,
    dz_ref,
    dzt_ref,
    sqz_ref,
    pxy_ref,
    pxyt_ref,
    pz_ref,
    out_ref,
    coarse_ref,
    fbuf,
    xs,
    ys,
    xr,
    yr,
    dr,
    onehot,
    csend,
    crecv,
    psend,
    precv,
    send_sem,
    recv_sem,
    csend_sem,
    crecv_sem,
    psend_sem,
    precv_sem,
):
    nw, nn, sx, sy, sz, slots, padded = sizes
    rows = sx * sy
    w, n = lax.axis_index("wide"), lax.axis_index("narrow")
    ez = sz // NODES
    pairs = (sx // NODES) * (sy // NODES)

    def exists(step):
        dw, dn = step
        cond = None
        for place, move, count in ((w, dw, nw), (n, dn, nn)):
            if move:
                here = place > 0 if move < 0 else place < count - 1
                cond = here if cond is None else jnp.logical_and(cond, here)
        return cond

    barrier = pltpu.get_barrier_semaphore()
    for step in DIRS[:6]:

        @pl.when(exists(step))
        def _():
            pl.semaphore_signal(
                barrier, inc=1, device_id=(w + step[0], n + step[1]), device_id_type=MESH
            )

    for j in range(1, nn):
        pl.semaphore_signal(
            barrier, inc=1, device_id=(w, lax.rem(n + j, nn)), device_id_type=MESH
        )

    def barrier_wait():
        peers = nn - 1
        for step in DIRS[:6]:
            peers = peers + jnp.where(exists(step), 1, 0)
        pl.semaphore_wait(barrier, peers)

    def buffers(field, k):
        dw, dn = DIRS[k]
        xside, yside = int(dw > 0), int(dn > 0)
        o = OPPOSITE[k]
        if dn == 0:
            return xs.at[field, xside], xr.at[field, int(DIRS[o][0] > 0)]
        if dw == 0:
            return ys.at[field, yside], yr.at[field, int(DIRS[o][1] > 0)]
        line = sy - 1 if dn > 0 else 0
        return xs.at[field, xside, pl.ds(line, 1)], dr.at[field, o - 2]

    def descriptor(field, k):
        source, target = buffers(field, k)
        return pltpu.make_async_remote_copy(
            src_ref=source,
            dst_ref=target,
            send_sem=send_sem.at[field, k],
            recv_sem=recv_sem.at[field, OPPOSITE[k]],
            device_id=(w + DIRS[k][0], n + DIRS[k][1]),
            device_id_type=MESH,
        )

    lane = lax.broadcasted_iota(jnp.int32, (1, sz), 1)
    z_low = jnp.logical_and(lane % NODES == 0, lane > 0)
    z_high = jnp.logical_and(lane % NODES == NODES - 1, lane < sz - 1)
    sub = lax.broadcasted_iota(jnp.int32, (1, NODES, 1), 1)

    def local_sum(value):
        value = (
            value
            + jnp.where(z_low, pltpu.roll(value, 1, 1), 0.0)
            + jnp.where(z_high, pltpu.roll(value, sz - 1, 1), 0.0)
        )
        cube = value.reshape(sx, sy // NODES, NODES, sz)
        parts = []
        count = sy // NODES
        for e in range(count):
            block = cube[:, e]
            if e > 0:
                block = block + jnp.where(sub == 0, pltpu.roll(cube[:, e - 1], 1, 1), 0.0)
            if e < count - 1:
                block = block + jnp.where(
                    sub == NODES - 1, pltpu.roll(cube[:, e + 1], NODES - 1, 1), 0.0
                )
            parts.append(block)
        cube = jnp.stack(parts, axis=1).reshape(sx, sy, sz)
        planes = []
        for x in range(sx):
            plane = cube[x]
            if x % NODES == 0 and x > 0:
                plane = plane + cube[x - 1]
            if x % NODES == NODES - 1 and x < sx - 1:
                plane = plane + cube[x + 1]
            planes.append(plane)
        return jnp.stack(planes, axis=0).reshape(rows, sz)

    def prepare(field, value):
        value = local_sum(value)
        xs[field, 0] = value[:sy]
        xs[field, 1] = value[rows - sy :]
        fbuf[field] = value
        ys[field, 0] = fbuf[field, pl.ds(0, sx, stride=sy), :]
        ys[field, 1] = fbuf[field, pl.ds(sy - 1, sx, stride=sy), :]

    def send(field):
        for k, step in enumerate(DIRS):

            @pl.when(exists(step))
            def _():
                descriptor(field, k).start()

    def finish(field):
        for k in (6, 7, 0, 1, 2, 3, 4, 5):
            dw, dn = DIRS[k]

            @pl.when(exists(DIRS[k]))
            def _():
                descriptor(field, OPPOSITE[k]).wait_recv()
                first = 0 if dw < 0 else rows - sy
                if dn == 0:
                    fbuf[field, pl.ds(first, sy), :] += xr[field, int(dw > 0)]
                elif dw == 0:
                    line = 0 if dn < 0 else sy - 1
                    fbuf[field, pl.ds(line, sx, stride=sy), :] += yr[field, int(dn > 0)]
                else:
                    line = first + (0 if dn < 0 else sy - 1)
                    fbuf[field, pl.ds(line, 1), :] += dr[field, k - 2]

        return fbuf[field]

    def along_x(value, matrix):
        cube = value.reshape(sx // NODES, NODES, sy, sz)
        out = []
        for a in range(NODES):
            total = None
            for b in range(NODES):
                entry = float(matrix[a, b])
                if entry == 0.0:
                    continue
                term = entry * cube[:, b]
                total = term if total is None else total + term
            out.append(total)
        return jnp.stack(out, axis=1).reshape(rows, sz)

    def element_operator(value):
        gx = along_x(value, derivative) * geo_ref[0]
        gy = left(dy_ref, value) * geo_ref[1]
        gz = right(value, dz_ref) * geo_ref[2]
        return (
            along_x(gx, derivative.T)
            + left(dyt_ref, gy)
            + right(gz, dzt_ref)
            + hel_ref[...] * value
        )

    prepare(RES, res_ref[...])
    square = derivative * derivative
    prepare(
        DIAG,
        along_x(geo_ref[0], square.T)
        + left(sqy_ref, geo_ref[1])
        + right(geo_ref[2], sqz_ref)
        + hel_ref[...],
    )
    csend[...] = cc_ref[...]
    barrier_wait()

    def coarse_copy(source, target, sems, rsems, j):
        peer = lax.rem(n + j, nn)
        return pltpu.make_async_remote_copy(
            src_ref=source,
            dst_ref=target,
            send_sem=sems.at[j],
            recv_sem=rsems.at[j],
            device_id=(w, peer),
            device_id_type=MESH,
        )

    for j in range(1, nn):
        coarse_copy(csend, crecv.at[j], csend_sem, crecv_sem, j).start()
    send(DIAG)
    send(RES)

    lanes = lax.broadcasted_iota(jnp.int32, (1, padded), 1)
    values = []
    for j in range(nn):
        owner = lax.rem(n - j + nn, nn)
        values.append(jnp.where(lanes < slots, owner * slots + lanes, -1))
    numbers = jnp.concatenate(values, axis=1)
    for pair in range(pairs):
        block = ids_ref[pair].T
        for v in range(8):
            onehot[pl.ds((pair * 8 + v) * ez, ez), :] = jnp.where(
                block[:, v : v + 1] == numbers, 1.0, 0.0
            ).astype(jnp.bfloat16)

    pieces = [csend[...]]
    for j in range(1, nn):
        coarse_copy(csend, crecv.at[j], csend_sem, crecv_sem, j).wait_recv()
        pieces.append(crecv[j])
    whole = jnp.concatenate(pieces, axis=1)
    contract_last = (((1,), (1,)), ((), ()))
    picked = jnp.sum(
        lax.dot_general(
            three_rows(whole), onehot[...], contract_last, preferred_element_type=jnp.float32
        ),
        axis=0,
        keepdims=True,
    )
    columns = pairs * 8 * ez
    groups = pairs * 4
    row_of = lax.broadcasted_iota(jnp.int32, (groups, columns), 1) // (2 * ez)
    mine = row_of == lax.broadcasted_iota(jnp.int32, (groups, columns), 0)
    spread = jnp.where(mine, picked, 0.0)
    along_z = jnp.dot(
        spread, pz_ref[...], precision=HIGHEST, preferred_element_type=jnp.float32
    )
    correction = jnp.dot(
        pxy_ref[...], along_z, precision=HIGHEST, preferred_element_type=jnp.float32
    )
    prepare(CORR, element_operator(correction))
    send(CORR)

    inverse = 1.0 / finish(DIAG)
    residual = finish(RES)

    theta = 0.5 * (high_bound + low_bound)
    delta = 0.5 * (high_bound - low_bound)
    sigma = theta / delta

    rho = 1.0 / sigma
    update = inverse * residual * (1.0 / theta)
    solution_value = correction
    for number in range(DEGREE):
        solution_value = solution_value + update
        field = FIRST + number
        prepare(field, element_operator(update))
        send(field)
        residual = residual - finish(field)
        if number + 1 < DEGREE:
            rho_next = 1.0 / (2.0 * sigma - rho)
            update = (rho_next * rho) * update + (2.0 * rho_next / delta) * inverse * residual
            rho = rho_next

    pre_residual = residual
    residual = residual - finish(CORR)
    rho = 1.0 / sigma
    update = inverse * residual * (1.0 / theta)
    for number in range(DEGREE):
        solution_value = solution_value + update
        if number < DEGREE - 1:
            field = FIRST + DEGREE + number
            prepare(field, element_operator(update))
            send(field)
            if number == 0:
                point = lax.broadcasted_iota(jnp.int32, (rows, sz), 0)
                x, y = point // sy, point % sy
                z = lax.broadcasted_iota(jnp.int32, (rows, sz), 1)
                weighted = pre_residual
                for local, start, total in (
                    (x, w * sx, nw * sx),
                    (y, n * sy, nn * sy),
                    (z, 0, sz),
                ):
                    spot = start + local
                    inner = jnp.logical_or(
                        jnp.logical_and(local % NODES == 0, spot > 0),
                        jnp.logical_and(local % NODES == NODES - 1, spot < total - 1),
                    )
                    weighted = weighted * jnp.where(inner, 0.5, 1.0)
                on_xy = jnp.dot(
                    pxyt_ref[...], weighted, precision=HIGHEST, preferred_element_type=jnp.float32
                )
                on_z = lax.dot_general(
                    on_xy,
                    pz_ref[...],
                    contract_last,
                    precision=HIGHEST,
                    preferred_element_type=jnp.float32,
                )
                corners = jnp.sum(jnp.where(mine, on_z, 0.0), axis=0, keepdims=True)
                partial = jnp.sum(dot(three_rows(corners), onehot[...]), axis=0, keepdims=True)
                for j in range(1, nn):
                    at = (nn - j) * padded
                    psend[j] = partial[:, at : at + padded]
                    coarse_copy(psend.at[j], precv.at[j], psend_sem, precv_sem, j).start()
                own = partial[:, :padded]
            residual = residual - finish(field)
            rho_next = 1.0 / (2.0 * sigma - rho)
            update = (rho_next * rho) * update + (2.0 * rho_next / delta) * inverse * residual
            rho = rho_next
    out_ref[...] = solution_value

    for j in range(1, nn):
        coarse_copy(psend.at[j], precv.at[j], psend_sem, precv_sem, j).wait_recv()
        own = own + precv[j]
    coarse_ref[...] = own

    for j in range(1, nn):
        coarse_copy(csend, crecv.at[j], csend_sem, crecv_sem, j).wait_send()
        coarse_copy(psend.at[j], precv.at[j], psend_sem, precv_sem, j).wait_send()
    for field in range(FIELDS):
        for k, step in enumerate(DIRS):

            @pl.when(exists(step))
            def _():
                descriptor(field, k).wait_send()


def on_device(nw, nn, residual_local, geometry, helmholtz, coarse_ids, coarse_correction):
    derivative, linear = tables()
    sx, sy, sz = residual_local.shape
    rows = sx * sy
    slots = coarse_correction.shape[0]
    padded = -(-slots // 128) * 128
    ex, ey, ez = sx // NODES, sy // NODES, sz // NODES
    pairs = ex * ey
    square = derivative * derivative
    eye_y, eye_z = np.eye(rows // NODES), np.eye(ez)

    pxy = np.einsum("eE,ia,fF,jb->eifjEFab", np.eye(ex), linear, np.eye(ey), linear)
    pxy = pxy.reshape(rows, pairs * 4).astype(np.float32)
    pz = np.einsum("kc,eE->cEek", linear, eye_z).reshape(2 * ez, sz)
    pz = np.tile(pz, (pairs * 4, 1)).astype(np.float32)

    constants = (
        left_table(np.kron(eye_y, derivative)),
        left_table(np.kron(eye_y, derivative.T)),
        left_table(np.kron(eye_y, square.T)),
        right_table(np.kron(eye_z, derivative.T)),
        right_table(np.kron(eye_z, derivative)),
        right_table(np.kron(eye_z, square)),
        pxy,
        np.ascontiguousarray(pxy.T),
        pz,
    )
    coarse_row = coarse_correction.reshape(1, slots)
    if padded != slots:
        coarse_row = jnp.pad(coarse_row, ((0, 0), (0, padded - slots)))

    f32 = jnp.float32
    dma = pltpu.SemaphoreType.DMA
    vmem = pl.BlockSpec(memory_space=pltpu.VMEM)
    out, coarse = pl.pallas_call(
        functools.partial(kernel, (nw, nn, sx, sy, sz, slots, padded), derivative),
        out_shape=(
            jax.ShapeDtypeStruct((rows, sz), f32),
            jax.ShapeDtypeStruct((1, padded), f32),
        ),
        in_specs=[vmem] * 14,
        out_specs=(vmem, vmem),
        scratch_shapes=[
            pltpu.VMEM((FIELDS, rows, sz), f32),
            pltpu.VMEM((FIELDS, 2, sy, sz), f32),
            pltpu.VMEM((FIELDS, 2, sx, sz), f32),
            pltpu.VMEM((FIELDS, 2, sy, sz), f32),
            pltpu.VMEM((FIELDS, 2, sx, sz), f32),
            pltpu.VMEM((FIELDS, 4, 1, sz), f32),
            pltpu.VMEM((pairs * 8 * ez, nn * padded), jnp.bfloat16),
            pltpu.VMEM((1, padded), f32),
            pltpu.VMEM((nn, 1, padded), f32),
            pltpu.VMEM((nn, 1, padded), f32),
            pltpu.VMEM((nn, 1, padded), f32),
            dma((FIELDS, len(DIRS))),
            dma((FIELDS, len(DIRS))),
            dma((nn,)),
            dma((nn,)),
            dma((nn,)),
            dma((nn,)),
        ],
        compiler_params=pltpu.CompilerParams(collective_id=0, has_side_effects=True),
    )(
        residual_local.reshape(rows, sz),
        geometry.reshape(3, rows, sz),
        helmholtz.reshape(rows, sz),
        coarse_ids.transpose(0, 1, 3, 2).reshape(pairs, 8, ez),
        coarse_row,
        *[jnp.asarray(c) for c in constants],
    )
    return out.reshape(sx, sy, sz), coarse[:, :slots].reshape(slots)


def solution(mesh):
    return jax.shard_map(
        functools.partial(on_device, mesh.shape["wide"], mesh.shape["narrow"]),
        mesh=mesh,
        in_specs=(
            P("wide", "narrow", None),
            P(None, "wide", "narrow", None),
            P("wide", "narrow", None),
            P("wide", "narrow", None, None),
            P(("wide", "narrow")),
        ),
        out_specs=(P("wide", "narrow", None), P(("wide", "narrow"))),
        check_vma=False,
    )
```

time: 124 us -> 33.7 us (0.27); the launches traced: 122 us -> 33 us
  starting transfers between devices: 48.8 us -> 0 us
  waiting for transfers between devices: 31.5 us -> 0 us
  Pallas kernels: 0 us -> 30.3 us
  matrix products: 12.4 us -> 0 us
  local copies, waits for them, and re-layouts: 13.9 us -> 2.08 us
  other arithmetic: 7.79 us -> 0 us
  blocking collectives: 5.2 us -> 0 us
  between operations: 2.41 us -> 0.65 us
    ppermute x24 -> x0, starting transfers between devices: 48.8 us -> none  [the longest x12 33.1 us: with_halo(): lax.ppermute(lax.slice_in_dim(block, block.shape[dim] - width, None, axis...]
    ppermute x24 -> x0, waiting for transfers between devices: 31.5 us -> none  [the longest x12 31.2 us: with_halo(): lax.ppermute(lax.slice_in_dim(block, 0, width, axis=dim), axis, backward)]
    pallas_call x0 -> x1, Pallas kernels: none -> 30.3 us  [on_device(): pl.pallas_call(functools.partial(kernel, (nw, nn, sx, sy, sz, slots, padd...]
    dot_general x45 -> x0, matrix products: 12.4 us -> none  [the longest x6 1.89 us: element_operator(): jnp.einsum('ab,eayz->ebyz', derivative, grads, precision=highest)]
    unnamed x29 -> x4, local copies, waits for them, and re-layouts: 7.38 us -> 2.08 us
    scatter-add x1 -> x0, other arithmetic: 4.09 us -> none  [on_device(): jax.ops.segment_sum(corners.reshape(-1), coarse_ids.reshape(-1), num_segm...]
    gather x1 -> x0, local copies, waits for them, and re-layouts: 3.5 us -> none  [on_device(): correction = prolong(whole[coarse_ids], linear, block, sx, sy, sz)]
    unnamed x1 -> x0, blocking collectives: 3.26 us -> none
  transfers between devices with their start and end apart: 24 -> 0, of which waited for: 12 -> 0; matrix products, arithmetic and copies ran while one was open for 6% -> 0% of each run, Pallas kernels for 0% -> 0%
where the time goes in v1:
time: 33.7 us; the launch traced here: 33 us
  Pallas kernels  30.3 us (90%)
  local copies, waits for them, and re-layouts  2.08 us (6%)
  between operations  0.65 us (2%)
    pallas_call x1, Pallas kernels, on_device(): pl.pallas_call(functools.partial(kernel, (nw, nn, sx, sy, sz, slots, padd...  30.3 us
    unnamed x4, local copies, waits for them, and re-layouts  2.08 us

profile of v1, /device:TPU:0, one launch (start us, length us, event | category | flops | bytes accessed | tf_op | source)
XLA Modules:
  0.0 33.0 jit_solution(10764690265065874522)
XLA Ops:
  0.6 30.3 %shard_map.149 = (f32[256,128]{1,0:T(8,128)}, f32[1,128]{1,0:T(1,128)}) custom-call(f32[256,128]{1,0:T(8,128)} %bitcast.10, f32[3,256,128]{2,1,0:T(8,128)} %bitcast.9, f32[256,128]{1,0:T(8,128)} %bitcast.11, s32[4,8,16]{2,1,0:T(8,128)} %bitcast.13, f32[1,128]{1,0:T(1,128)} %bitcast.14, bf16[2,256,256]{2,1,0:T(8,128)(2,1)} %constant.18.clone.dy_ref, ...), custom_call_target="tpu_custom_call" | custom-call | tf_op jit(solution)/shard_map/pallas_call | solution.py:492
  30.9 0.0 copy-start
  31.0 1.6 %copy.18 = f32[16,16,128]{2,1,0:T(8,128)} copy(f32[16,16,128]{2,1,0:T(8,128)} %bitcast.12) | data formatting | bytes 262144
  32.5 0.0 copy-done
  32.5 0.5 %copy.19 = f32[128]{0:T(128)} copy(f32[128]{0:T(128)S(1)} %bitcast.15) | data formatting | bytes 1024
Async XLA Ops:
  30.9 1.6 %copy-start = (f32[1,128]{1,0:T(1,128)S(1)}, f32[1,128]{1,0:T(1,128)}, u32[]{:S(2)}) copy-start(f32[1,128]{1,0:T(1,128)} %get-tuple-element.5) | copy-start | bytes 1540

commit v2 on v1

--- a/solution.py
+++ b/solution.py
@@ -26,6 +26,7 @@
 )
 
 DIRS = ((-1, 0), (1, 0), (-1, -1), (-1, 1), (1, -1), (1, 1), (0, -1), (0, 1))
+X_DIRS, Y_DIRS = (0, 1, 2, 3, 4, 5), (6, 7)
 OPPOSITE = tuple(DIRS.index((-a, -b)) for a, b in DIRS)
 
 DIAG, RES, CORR, FIRST = 0, 1, 2, 3
@@ -139,6 +140,9 @@
     xr,
     yr,
     dr,
+    gm,
+    tsend,
+    trecv,
     onehot,
     csend,
     crecv,
@@ -150,6 +154,8 @@
     crecv_sem,
     psend_sem,
     precv_sem,
+    tsend_sem,
+    trecv_sem,
 ):
     nw, nn, sx, sy, sz, slots, padded = sizes
     rows = sx * sy
@@ -213,13 +219,13 @@
     z_high = jnp.logical_and(lane % NODES == NODES - 1, lane < sz - 1)
     sub = lax.broadcasted_iota(jnp.int32, (1, NODES, 1), 1)
 
-    def local_sum(value):
+    def sum_yz(value):
         value = (
             value
             + jnp.where(z_low, pltpu.roll(value, 1, 1), 0.0)
             + jnp.where(z_high, pltpu.roll(value, sz - 1, 1), 0.0)
         )
-        cube = value.reshape(sx, sy // NODES, NODES, sz)
+        cube = value.reshape(value.shape[0] // sy, sy // NODES, NODES, sz)
         parts = []
         count = sy // NODES
         for e in range(count):
@@ -231,7 +237,10 @@
                     sub == NODES - 1, pltpu.roll(cube[:, e + 1], NODES - 1, 1), 0.0
                 )
             parts.append(block)
-        cube = jnp.stack(parts, axis=1).reshape(sx, sy, sz)
+        return jnp.stack(parts, axis=1).reshape(value.shape)
+
+    def local_sum(value):
+        cube = sum_yz(value).reshape(sx, sy, sz)
         planes = []
         for x in range(sx):
             plane = cube[x]
@@ -242,23 +251,24 @@
             planes.append(plane)
         return jnp.stack(planes, axis=0).reshape(rows, sz)
 
-    def prepare(field, value):
+    def prepare(field, value, with_faces):
         value = local_sum(value)
-        xs[field, 0] = value[:sy]
-        xs[field, 1] = value[rows - sy :]
+        if with_faces:
+            xs[field, 0] = value[:sy]
+            xs[field, 1] = value[rows - sy :]
         fbuf[field] = value
         ys[field, 0] = fbuf[field, pl.ds(0, sx, stride=sy), :]
         ys[field, 1] = fbuf[field, pl.ds(sy - 1, sx, stride=sy), :]
 
-    def send(field):
-        for k, step in enumerate(DIRS):
-
-            @pl.when(exists(step))
+    def send(field, ks):
+        for k in ks:
+
+            @pl.when(exists(DIRS[k]))
             def _():
                 descriptor(field, k).start()
 
-    def finish(field):
-        for k in (6, 7, 0, 1, 2, 3, 4, 5):
+    def finish(field, ks):
+        for k in ks:
             dw, dn = DIRS[k]
 
             @pl.when(exists(DIRS[k]))
@@ -274,7 +284,50 @@
                     line = first + (0 if dn < 0 else sy - 1)
                     fbuf[field, pl.ds(line, 1), :] += dr[field, k - 2]
 
-        return fbuf[field]
+    def patch(value, faces):
+        return jnp.concatenate([faces[:sy], value[sy : rows - sy], faces[sy:]], axis=0)
+
+    def faces_of(value):
+        return jnp.concatenate([value[:sy], value[rows - sy :]], axis=0)
+
+    def face_part(field):
+        return jnp.concatenate(
+            [fbuf[field, pl.ds(0, sy), :], fbuf[field, pl.ds(rows - sy, sy), :]], axis=0
+        )
+
+    def inner_terms(field, value):
+        planes = []
+        for base, face in ((0, 0), (sx - NODES, NODES - 1)):
+            total = None
+            for a in range(NODES):
+                inner = None
+                for b in range(NODES):
+                    entry = float(derivative[a, b])
+                    if b == face or entry == 0.0:
+                        continue
+                    term = entry * value[(base + b) * sy : (base + b + 1) * sy]
+                    inner = term if inner is None else inner + term
+                entry = float(derivative[a, face])
+                if inner is None or entry == 0.0:
+                    continue
+                term = entry * geo_ref[0, pl.ds((base + a) * sy, sy), :] * inner
+                total = term if total is None else total + term
+            planes.append(total)
+        both = sum_yz(jnp.concatenate(planes, axis=0))
+        xs[field, 0] = both[:sy]
+        xs[field, 1] = both[sy:]
+        send(field, X_DIRS)
+
+    def table_copy(k):
+        o = OPPOSITE[k]
+        return pltpu.make_async_remote_copy(
+            src_ref=tsend.at[k],
+            dst_ref=trecv.at[o],
+            send_sem=tsend_sem.at[k],
+            recv_sem=trecv_sem.at[o],
+            device_id=(w + DIRS[k][0], n),
+            device_id_type=MESH,
+        )
 
     def along_x(value, matrix):
         cube = value.reshape(sx // NODES, NODES, sy, sz)
@@ -290,45 +343,33 @@
             out.append(total)
         return jnp.stack(out, axis=1).reshape(rows, sz)
 
-    def element_operator(value):
+    def element_operator(value, second, third, mass):
         gx = along_x(value, derivative) * geo_ref[0]
-        gy = left(dy_ref, value) * geo_ref[1]
-        gz = right(value, dz_ref) * geo_ref[2]
+        gy = left(dy_ref, value) * second[...]
+        gz = right(value, dz_ref) * third[...]
         return (
             along_x(gx, derivative.T)
             + left(dyt_ref, gy)
             + right(gz, dzt_ref)
-            + hel_ref[...] * value
-        )
-
-    prepare(RES, res_ref[...])
+            + mass[...] * value
+        )
+
+    def with_neighbours(value):
+        return element_operator(value, gm.at[0], gm.at[1], gm.at[2])
+
+    prepare(RES, res_ref[...], True)
     square = derivative * derivative
+    diagonal_x = along_x(geo_ref[0], square.T)
+    for side, first in ((0, 0), (1, rows - sy)):
+        tsend[side, 0] = geo_ref[1, pl.ds(first, sy), :]
+        tsend[side, 1] = geo_ref[2, pl.ds(first, sy), :]
+        tsend[side, 2] = diagonal_x[first : first + sy] + hel_ref[pl.ds(first, sy), :]
     prepare(
         DIAG,
-        along_x(geo_ref[0], square.T)
-        + left(sqy_ref, geo_ref[1])
-        + right(geo_ref[2], sqz_ref)
-        + hel_ref[...],
+        diagonal_x + left(sqy_ref, geo_ref[1]) + right(geo_ref[2], sqz_ref) + hel_ref[...],
+        True,
     )
     csend[...] = cc_ref[...]
-    barrier_wait()
-
-    def coarse_copy(source, target, sems, rsems, j):
-        peer = lax.rem(n + j, nn)
-        return pltpu.make_async_remote_copy(
-            src_ref=source,
-            dst_ref=target,
-            send_sem=sems.at[j],
-            recv_sem=rsems.at[j],
-            device_id=(w, peer),
-            device_id_type=MESH,
-        )
-
-    for j in range(1, nn):
-        coarse_copy(csend, crecv.at[j], csend_sem, crecv_sem, j).start()
-    send(DIAG)
-    send(RES)
-
     lanes = lax.broadcasted_iota(jnp.int32, (1, padded), 1)
     values = []
     for j in range(nn):
@@ -342,6 +383,42 @@
                 block[:, v : v + 1] == numbers, 1.0, 0.0
             ).astype(jnp.bfloat16)
 
+    barrier_wait()
+
+    def coarse_copy(source, target, sems, rsems, j):
+        peer = lax.rem(n + j, nn)
+        return pltpu.make_async_remote_copy(
+            src_ref=source,
+            dst_ref=target,
+            send_sem=sems.at[j],
+            recv_sem=rsems.at[j],
+            device_id=(w, peer),
+            device_id_type=MESH,
+        )
+
+    for j in range(1, nn):
+        coarse_copy(csend, crecv.at[j], csend_sem, crecv_sem, j).start()
+    send(DIAG, Y_DIRS)
+    send(RES, Y_DIRS)
+    send(DIAG, X_DIRS)
+    send(RES, X_DIRS)
+    for k in (0, 1):
+
+        @pl.when(exists(DIRS[k]))
+        def _():
+            table_copy(k).start()
+
+    theta = 0.5 * (high_bound + low_bound)
+    delta = 0.5 * (high_bound - low_bound)
+    sigma = theta / delta
+
+    finish(DIAG, Y_DIRS)
+    finish(RES, Y_DIRS)
+    inverse = 1.0 / fbuf[DIAG]
+    residual = fbuf[RES]
+    update = inverse * residual * (1.0 / theta)
+    inner_terms(FIRST, update)
+
     pieces = [csend[...]]
     for j in range(1, nn):
         coarse_copy(csend, crecv.at[j], csend_sem, crecv_sem, j).wait_recv()
@@ -366,77 +443,100 @@
     correction = jnp.dot(
         pxy_ref[...], along_z, precision=HIGHEST, preferred_element_type=jnp.float32
     )
-    prepare(CORR, element_operator(correction))
-    send(CORR)
-
-    inverse = 1.0 / finish(DIAG)
-    residual = finish(RES)
-
-    theta = 0.5 * (high_bound + low_bound)
-    delta = 0.5 * (high_bound - low_bound)
-    sigma = theta / delta
+    prepare(CORR, element_operator(correction, geo_ref.at[1], geo_ref.at[2], hel_ref), True)
+    send(CORR, (*Y_DIRS, *X_DIRS))
+
+    gm[0] = geo_ref[1]
+    gm[1] = geo_ref[2]
+    gm[2] = hel_ref[...]
+    for k, first in ((0, 0), (1, rows - sy)):
+
+        @pl.when(exists(DIRS[k]))
+        def _():
+            table_copy(OPPOSITE[k]).wait_recv()
+            for part in range(3):
+                gm[part, pl.ds(first, sy), :] += trecv[k, part]
+
+    finish(DIAG, X_DIRS)
+    finish(RES, X_DIRS)
+    inverse_faces = 1.0 / face_part(DIAG)
+    residual_faces = face_part(RES)
+    inverse = patch(inverse, inverse_faces)
+    residual = patch(residual, residual_faces)
+    update = patch(update, inverse_faces * residual_faces * (1.0 / theta))
 
     rho = 1.0 / sigma
-    update = inverse * residual * (1.0 / theta)
     solution_value = correction
-    for number in range(DEGREE):
+    count = 2 * DEGREE - 1
+    for number in range(count):
         solution_value = solution_value + update
         field = FIRST + number
-        prepare(field, element_operator(update))
-        send(field)
-        residual = residual - finish(field)
-        if number + 1 < DEGREE:
+        prepare(field, with_neighbours(update), False)
+        send(field, Y_DIRS)
+        if number == DEGREE - 1:
+            finish(CORR, (*Y_DIRS, *X_DIRS))
+        finish(field, Y_DIRS)
+
+        old_residual, old_update = residual, update
+        residual = old_residual - fbuf[field]
+        if number == DEGREE - 1:
+            image = fbuf[CORR]
+            shifted = residual - image
+            update = inverse * shifted * (1.0 / theta)
+        else:
             rho_next = 1.0 / (2.0 * sigma - rho)
-            update = (rho_next * rho) * update + (2.0 * rho_next / delta) * inverse * residual
+            keep, gain = rho_next * rho, 2.0 * rho_next / delta
             rho = rho_next
-
-    pre_residual = residual
-    residual = residual - finish(CORR)
-    rho = 1.0 / sigma
-    update = inverse * residual * (1.0 / theta)
-    for number in range(DEGREE):
-        solution_value = solution_value + update
-        if number < DEGREE - 1:
-            field = FIRST + DEGREE + number
-            prepare(field, element_operator(update))
-            send(field)
-            if number == 0:
-                point = lax.broadcasted_iota(jnp.int32, (rows, sz), 0)
-                x, y = point // sy, point % sy
-                z = lax.broadcasted_iota(jnp.int32, (rows, sz), 1)
-                weighted = pre_residual
-                for local, start, total in (
-                    (x, w * sx, nw * sx),
-                    (y, n * sy, nn * sy),
-                    (z, 0, sz),
-                ):
-                    spot = start + local
-                    inner = jnp.logical_or(
-                        jnp.logical_and(local % NODES == 0, spot > 0),
-                        jnp.logical_and(local % NODES == NODES - 1, spot < total - 1),
-                    )
-                    weighted = weighted * jnp.where(inner, 0.5, 1.0)
-                on_xy = jnp.dot(
-                    pxyt_ref[...], weighted, precision=HIGHEST, preferred_element_type=jnp.float32
+            update = keep * old_update + gain * inverse * residual
+        if number + 1 < count:
+            inner_terms(field + 1, update)
+        if number == DEGREE:
+            point = lax.broadcasted_iota(jnp.int32, (rows, sz), 0)
+            x, y = point // sy, point % sy
+            z = lax.broadcasted_iota(jnp.int32, (rows, sz), 1)
+            weighted = pre_residual
+            for local, start, total in (
+                (x, w * sx, nw * sx),
+                (y, n * sy, nn * sy),
+                (z, 0, sz),
+            ):
+                spot = start + local
+                inner = jnp.logical_or(
+                    jnp.logical_and(local % NODES == 0, spot > 0),
+                    jnp.logical_and(local % NODES == NODES - 1, spot < total - 1),
                 )
-                on_z = lax.dot_general(
-                    on_xy,
-                    pz_ref[...],
-                    contract_last,
-                    precision=HIGHEST,
-                    preferred_element_type=jnp.float32,
-                )
-                corners = jnp.sum(jnp.where(mine, on_z, 0.0), axis=0, keepdims=True)
-                partial = jnp.sum(dot(three_rows(corners), onehot[...]), axis=0, keepdims=True)
-                for j in range(1, nn):
-                    at = (nn - j) * padded
-                    psend[j] = partial[:, at : at + padded]
-                    coarse_copy(psend.at[j], precv.at[j], psend_sem, precv_sem, j).start()
-                own = partial[:, :padded]
-            residual = residual - finish(field)
-            rho_next = 1.0 / (2.0 * sigma - rho)
-            update = (rho_next * rho) * update + (2.0 * rho_next / delta) * inverse * residual
-            rho = rho_next
+                weighted = weighted * jnp.where(inner, 0.5, 1.0)
+            on_xy = jnp.dot(
+                pxyt_ref[...], weighted, precision=HIGHEST, preferred_element_type=jnp.float32
+            )
+            on_z = lax.dot_general(
+                on_xy,
+                pz_ref[...],
+                contract_last,
+                precision=HIGHEST,
+                preferred_element_type=jnp.float32,
+            )
+            corners = jnp.sum(jnp.where(mine, on_z, 0.0), axis=0, keepdims=True)
+            partial = jnp.sum(dot(three_rows(corners), onehot[...]), axis=0, keepdims=True)
+            for j in range(1, nn):
+                at = (nn - j) * padded
+                psend[j] = partial[:, at : at + padded]
+                coarse_copy(psend.at[j], precv.at[j], psend_sem, precv_sem, j).start()
+            own = partial[:, :padded]
+        finish(field, X_DIRS)
+        residual_faces = faces_of(old_residual) - face_part(field)
+        residual = patch(residual, residual_faces)
+        if number == DEGREE - 1:
+            pre_residual = residual
+            shifted_faces = residual_faces - faces_of(image)
+            residual = patch(shifted, shifted_faces)
+            update = patch(update, inverse_faces * shifted_faces * (1.0 / theta))
+            rho = 1.0 / sigma
+        else:
+            update = patch(
+                update, keep * faces_of(old_update) + gain * inverse_faces * residual_faces
+            )
+    solution_value = solution_value + update
     out_ref[...] = solution_value
 
     for j in range(1, nn):
@@ -453,6 +553,12 @@
             @pl.when(exists(step))
             def _():
                 descriptor(field, k).wait_send()
+
+    for k in (0, 1):
+
+        @pl.when(exists(DIRS[k]))
+        def _():
+            table_copy(k).wait_send()
 
 
 def on_device(nw, nn, residual_local, geometry, helmholtz, coarse_ids, coarse_correction):
@@ -504,6 +610,9 @@
             pltpu.VMEM((FIELDS, 2, sy, sz), f32),
             pltpu.VMEM((FIELDS, 2, sx, sz), f32),
             pltpu.VMEM((FIELDS, 4, 1, sz), f32),
+            pltpu.VMEM((3, rows, sz), f32),
+            pltpu.VMEM((2, 3, sy, sz), f32),
+            pltpu.VMEM((2, 3, sy, sz), f32),
             pltpu.VMEM((pairs * 8 * ez, nn * padded), jnp.bfloat16),
             pltpu.VMEM((1, padded), f32),
             pltpu.VMEM((nn, 1, padded), f32),
@@ -515,6 +624,8 @@
             dma((nn,)),
             dma((nn,)),
             dma((nn,)),
+            dma((2,)),
+            dma((2,)),
         ],
         compiler_params=pltpu.CompilerParams(collective_id=0, has_side_effects=True),
     )(

time: 33.7 us -> 25.1 us (0.74); the launches traced: 33 us -> 25 us
  Pallas kernels: 30.3 us -> 22.2 us
    pallas_call x1, Pallas kernels: 30.3 us -> 22.2 us  [on_device(): pl.pallas_call(functools.partial(kernel, (nw, nn, sx, sy, sz, slots, padd...]
where the time goes in v2:
time: 25.1 us; the launch traced here: 25 us
  Pallas kernels  22.2 us (88%)
  local copies, waits for them, and re-layouts  2.08 us (8%)
  between operations  0.65 us (3%)
    pallas_call x1, Pallas kernels, on_device(): pl.pallas_call(functools.partial(kernel, (nw, nn, sx, sy, sz, slots, padd...  22.2 us
    unnamed x4, local copies, waits for them, and re-layouts  2.08 us

profile of v2, /device:TPU:0, one launch (start us, length us, event | category | flops | bytes accessed | tf_op | source)
XLA Modules:
  0.0 25.0 jit_solution(9553483979925014769)
XLA Ops:
  0.6 22.2 %shard_map.149 = (f32[256,128]{1,0:T(8,128)}, f32[1,128]{1,0:T(1,128)}) custom-call(f32[256,128]{1,0:T(8,128)} %bitcast.10, f32[3,256,128]{2,1,0:T(8,128)} %bitcast.9, f32[256,128]{1,0:T(8,128)} %bitcast.11, s32[4,8,16]{2,1,0:T(8,128)} %bitcast.13, f32[1,128]{1,0:T(1,128)} %bitcast.14, bf16[2,256,256]{2,1,0:T(8,128)(2,1)} %constant.18.clone.dy_ref, ...), custom_call_target="tpu_custom_call" | custom-call | tf_op jit(solution)/shard_map/pallas_call | solution.py:598
  22.9 0.0 copy-start
  22.9 1.6 %copy.18 = f32[16,16,128]{2,1,0:T(8,128)} copy(f32[16,16,128]{2,1,0:T(8,128)} %bitcast.12) | data formatting | bytes 262144
  24.4 0.0 copy-done
  24.4 0.5 %copy.19 = f32[128]{0:T(128)} copy(f32[128]{0:T(128)S(1)} %bitcast.15) | data formatting | bytes 1024
Async XLA Ops:
  22.9 1.6 %copy-start = (f32[1,128]{1,0:T(1,128)S(1)}, f32[1,128]{1,0:T(1,128)}, u32[]{:S(2)}) copy-start(f32[1,128]{1,0:T(1,128)} %get-tuple-element.5) | copy-start | bytes 1540

commit v3 on v2

--- a/solution.py
+++ b/solution.py
@@ -103,6 +103,9 @@
     return both[:, :n] + both[:, n:]
 
 
+ORDER = ("hel", "res", "geo", "sqz", "sqy", "ids", "pz", "pxy", "dz", "dy", "dzt", "dyt", "pxyt")
+
+
 def three_rows(row):
     high = row.astype(jnp.bfloat16).astype(jnp.float32)
     rest = row - high
@@ -118,22 +121,23 @@
 def kernel(
     sizes,
     derivative,
-    res_ref,
-    geo_ref,
-    hel_ref,
-    ids_ref,
     cc_ref,
-    dy_ref,
-    dyt_ref,
-    sqy_ref,
-    dz_ref,
-    dzt_ref,
-    sqz_ref,
-    pxy_ref,
-    pxyt_ref,
-    pz_ref,
+    *refs,
+):
+    count = len(ORDER)
+    outside, (out_ref, coarse_ref), inside = refs[:count], refs[count : count + 2], refs[count + 2 :]
+    body(sizes, derivative, outside, cc_ref, out_ref, coarse_ref, inside[:count], *inside[count:])
+
+
+def body(
+    sizes,
+    derivative,
+    outside,
+    cc_ref,
     out_ref,
     coarse_ref,
+    inside,
+    load_sem,
     fbuf,
     xs,
     ys,
@@ -172,6 +176,20 @@
                 cond = here if cond is None else jnp.logical_and(cond, here)
         return cond
 
+    loads = {
+        name: pltpu.make_async_copy(outside[i], inside[i], load_sem.at[i])
+        for i, name in enumerate(ORDER)
+    }
+    at = dict(zip(ORDER, inside))
+    res_ref, geo_ref, hel_ref, ids_ref = at["res"], at["geo"], at["hel"], at["ids"]
+    dy_ref, dyt_ref, sqy_ref = at["dy"], at["dyt"], at["sqy"]
+    dz_ref, dzt_ref, sqz_ref = at["dz"], at["dzt"], at["sqz"]
+    pxy_ref, pxyt_ref, pz_ref = at["pxy"], at["pxyt"], at["pz"]
+
+    def loaded(*names):
+        for name in names:
+            loads[name].wait()
+
     barrier = pltpu.get_barrier_semaphore()
     for step in DIRS[:6]:
 
@@ -185,6 +203,9 @@
         pl.semaphore_signal(
             barrier, inc=1, device_id=(w, lax.rem(n + j, nn)), device_id_type=MESH
         )
+
+    for name in ORDER:
+        loads[name].start()
 
     def barrier_wait():
         peers = nn - 1
@@ -357,7 +378,9 @@
     def with_neighbours(value):
         return element_operator(value, gm.at[0], gm.at[1], gm.at[2])
 
+    loaded("hel", "res")
     prepare(RES, res_ref[...], True)
+    loaded("geo", "sqz", "sqy")
     square = derivative * derivative
     diagonal_x = along_x(geo_ref[0], square.T)
     for side, first in ((0, 0), (1, rows - sy)):
@@ -376,6 +399,7 @@
         owner = lax.rem(n - j + nn, nn)
         values.append(jnp.where(lanes < slots, owner * slots + lanes, -1))
     numbers = jnp.concatenate(values, axis=1)
+    loaded("ids")
     for pair in range(pairs):
         block = ids_ref[pair].T
         for v in range(8):
@@ -419,6 +443,7 @@
     update = inverse * residual * (1.0 / theta)
     inner_terms(FIRST, update)
 
+    loaded("pz", "pxy", "dz", "dy", "dzt", "dyt", "pxyt")
     pieces = [csend[...]]
     for j in range(1, nn):
         coarse_copy(csend, crecv.at[j], csend_sem, crecv_sem, j).wait_recv()
@@ -577,17 +602,22 @@
     pz = np.einsum("kc,eE->cEek", linear, eye_z).reshape(2 * ez, sz)
     pz = np.tile(pz, (pairs * 4, 1)).astype(np.float32)
 
-    constants = (
-        left_table(np.kron(eye_y, derivative)),
-        left_table(np.kron(eye_y, derivative.T)),
-        left_table(np.kron(eye_y, square.T)),
-        right_table(np.kron(eye_z, derivative.T)),
-        right_table(np.kron(eye_z, derivative)),
-        right_table(np.kron(eye_z, square)),
-        pxy,
-        np.ascontiguousarray(pxy.T),
-        pz,
-    )
+    operands = {
+        "res": residual_local.reshape(rows, sz),
+        "geo": geometry.reshape(3, rows, sz),
+        "hel": helmholtz.reshape(rows, sz),
+        "ids": coarse_ids.transpose(0, 1, 3, 2).reshape(pairs, 8, ez),
+        "dy": left_table(np.kron(eye_y, derivative)),
+        "dyt": left_table(np.kron(eye_y, derivative.T)),
+        "sqy": left_table(np.kron(eye_y, square.T)),
+        "dz": right_table(np.kron(eye_z, derivative.T)),
+        "dzt": right_table(np.kron(eye_z, derivative)),
+        "sqz": right_table(np.kron(eye_z, square)),
+        "pxy": pxy,
+        "pxyt": np.ascontiguousarray(pxy.T),
+        "pz": pz,
+    }
+    operands = [jnp.asarray(operands[name]) for name in ORDER]
     coarse_row = coarse_correction.reshape(1, slots)
     if padded != slots:
         coarse_row = jnp.pad(coarse_row, ((0, 0), (0, padded - slots)))
@@ -598,12 +628,14 @@
     out, coarse = pl.pallas_call(
         functools.partial(kernel, (nw, nn, sx, sy, sz, slots, padded), derivative),
         out_shape=(
-            jax.ShapeDtypeStruct((rows, sz), f32),
-            jax.ShapeDtypeStruct((1, padded), f32),
+            pltpu.VMEM((rows, sz), f32),
+            pltpu.VMEM((1, padded), f32),
         ),
-        in_specs=[vmem] * 14,
+        in_specs=[vmem] + [pl.BlockSpec(memory_space=pl.ANY)] * len(ORDER),
         out_specs=(vmem, vmem),
         scratch_shapes=[
+            *(pltpu.VMEM(o.shape, o.dtype) for o in operands),
+            dma((len(ORDER),)),
             pltpu.VMEM((FIELDS, rows, sz), f32),
             pltpu.VMEM((FIELDS, 2, sy, sz), f32),
             pltpu.VMEM((FIELDS, 2, sx, sz), f32),
@@ -629,12 +661,8 @@
         ],
         compiler_params=pltpu.CompilerParams(collective_id=0, has_side_effects=True),
     )(
-        residual_local.reshape(rows, sz),
-        geometry.reshape(3, rows, sz),
-        helmholtz.reshape(rows, sz),
-        coarse_ids.transpose(0, 1, 3, 2).reshape(pairs, 8, ez),
         coarse_row,
-        *[jnp.asarray(c) for c in constants],
+        *operands,
     )
     return out.reshape(sx, sy, sz), coarse[:, :slots].reshape(slots)
 

time: 25.1 us -> 22.8 us (0.908)
  Pallas kernels: 22.2 us -> 20.9 us
  local copies, waits for them, and re-layouts: 2.08 us -> 1.17 us
    pallas_call x1, Pallas kernels: 22.2 us -> 20.9 us  [on_device(): pl.pallas_call(functools.partial(kernel, (nw, nn, sx, sy, sz, slots, padd...]
    unnamed x4 -> x2, local copies, waits for them, and re-layouts: 2.08 us -> 1.17 us
where the time goes in v3:
time: 22.8 us; the launch traced here: 22.7 us
  Pallas kernels  20.9 us (92%)
  local copies, waits for them, and re-layouts  1.17 us (5%)
  between operations  0.64 us (3%)
    pallas_call x1, Pallas kernels, on_device(): pl.pallas_call(functools.partial(kernel, (nw, nn, sx, sy, sz, slots, padd...  20.9 us
    unnamed x2, local copies, waits for them, and re-layouts  1.17 us

profile of v3, /device:TPU:0, one launch (start us, length us, event | category | flops | bytes accessed | tf_op | source)
XLA Modules:
  0.0 22.7 jit_solution(9765757402443089419)
XLA Ops:
  0.6 20.9 %shard_map.149 = (f32[256,128]{1,0:T(8,128)S(1)}, f32[1,128]{1,0:T(1,128)S(1)}) custom-call(f32[1,128]{1,0:T(1,128)} %bitcast.15, f32[256,128]{1,0:T(8,128)} %bitcast.12, f32[256,128]{1,0:T(8,128)} %bitcast.13, f32[3,256,128]{2,1,0:T(8,128)} %bitcast.11, bf16[256,256]{1,0:T(8,128)(2,1)} %constant.18.clone.refs_3_, ...), custom_call_target="tpu_custom_call" | custom-call | tf_op jit(solution)/shard_map/pallas_call | solution.py:628
  21.5 0.7 %copy.18 = f32[16,16,128]{2,1,0:T(8,128)} copy(f32[16,16,128]{2,1,0:T(8,128)S(1)} %bitcast.9) | data formatting | bytes 262144
  22.2 0.5 %copy.19 = f32[128]{0:T(128)} copy(f32[128]{0:T(128)S(1)} %bitcast.10) | data formatting | bytes 1024

commit v4 on v3

--- a/solution.py
+++ b/solution.py
@@ -26,10 +26,10 @@
 )
 
 DIRS = ((-1, 0), (1, 0), (-1, -1), (-1, 1), (1, -1), (1, 1), (0, -1), (0, 1))
-X_DIRS, Y_DIRS = (0, 1, 2, 3, 4, 5), (6, 7)
+X_DIRS, Y_DIRS, X_ONLY = (0, 1, 2, 3, 4, 5), (6, 7), (0, 1)
 OPPOSITE = tuple(DIRS.index((-a, -b)) for a, b in DIRS)
 
-DIAG, RES, CORR, FIRST = 0, 1, 2, 3
+DIAG, RES, CORR, GEO_X, GEO_Y, GEO_Z, MASS, FIRST = range(8)
 FIELDS = FIRST + 2 * DEGREE - 1
 
 
@@ -63,6 +63,13 @@
     return derivative.astype(np.float32), linear.astype(np.float32)
 
 
+def chain(length):
+    matrix = np.eye(length)
+    for place in range(NODES, length, NODES):
+        matrix[place - 1, place] = matrix[place, place - 1] = 1.0
+    return matrix
+
+
 def halves(matrix):
     matrix = matrix.astype(np.float32)
     high = matrix.astype(jnp.bfloat16)
@@ -103,7 +110,15 @@
     return both[:, :n] + both[:, n:]
 
 
-ORDER = ("hel", "res", "geo", "sqz", "sqy", "ids", "pz", "pxy", "dz", "dy", "dzt", "dyt", "pxyt")
+def directions(field):
+    if field == GEO_X:
+        return Y_DIRS
+    if field == GEO_Y:
+        return X_ONLY
+    return (*X_ONLY, *Y_DIRS) if field >= FIRST else (*X_DIRS, *Y_DIRS)
+
+
+ORDER = ("hel", "res", "geo", "sqz", "sqy", "ids", "pz", "pxy", "dz", "dy", "dzt", "dyt", "pxyt", "sdzt", "sdyt")
 
 
 def three_rows(row):
@@ -144,7 +159,6 @@
     xr,
     yr,
     dr,
-    gm,
     tsend,
     trecv,
     onehot,
@@ -184,6 +198,7 @@
     res_ref, geo_ref, hel_ref, ids_ref = at["res"], at["geo"], at["hel"], at["ids"]
     dy_ref, dyt_ref, sqy_ref = at["dy"], at["dyt"], at["sqy"]
     dz_ref, dzt_ref, sqz_ref = at["dz"], at["dzt"], at["sqz"]
+    sdyt_ref, sdzt_ref = at["sdyt"], at["sdzt"]
     pxy_ref, pxyt_ref, pz_ref = at["pxy"], at["pxyt"], at["pz"]
 
     def loaded(*names):
@@ -240,13 +255,15 @@
     z_high = jnp.logical_and(lane % NODES == NODES - 1, lane < sz - 1)
     sub = lax.broadcasted_iota(jnp.int32, (1, NODES, 1), 1)
 
-    def sum_yz(value):
-        value = (
+    def sum_z(value):
+        return (
             value
             + jnp.where(z_low, pltpu.roll(value, 1, 1), 0.0)
             + jnp.where(z_high, pltpu.roll(value, sz - 1, 1), 0.0)
         )
-        cube = value.reshape(value.shape[0] // sy, sy // NODES, NODES, sz)
+
+    def sum_y(value):
+        cube = value.reshape(sx, sy // NODES, NODES, sz)
         parts = []
         count = sy // NODES
         for e in range(count):
@@ -258,10 +275,10 @@
                     sub == NODES - 1, pltpu.roll(cube[:, e + 1], NODES - 1, 1), 0.0
                 )
             parts.append(block)
-        return jnp.stack(parts, axis=1).reshape(value.shape)
-
-    def local_sum(value):
-        cube = sum_yz(value).reshape(sx, sy, sz)
+        return jnp.stack(parts, axis=1).reshape(rows, sz)
+
+    def sum_x(value):
+        cube = value.reshape(sx, sy, sz)
         planes = []
         for x in range(sx):
             plane = cube[x]
@@ -272,14 +289,17 @@
             planes.append(plane)
         return jnp.stack(planes, axis=0).reshape(rows, sz)
 
-    def prepare(field, value, with_faces):
-        value = local_sum(value)
-        if with_faces:
-            xs[field, 0] = value[:sy]
-            xs[field, 1] = value[rows - sy :]
+    def store_x(field, value):
+        xs[field, 0] = value[:sy]
+        xs[field, 1] = value[rows - sy :]
+
+    def prepare(field, value):
         fbuf[field] = value
-        ys[field, 0] = fbuf[field, pl.ds(0, sx, stride=sy), :]
-        ys[field, 1] = fbuf[field, pl.ds(sy - 1, sx, stride=sy), :]
+        if 0 in directions(field) and field < FIRST:
+            store_x(field, value)
+        if 6 in directions(field):
+            ys[field, 0] = fbuf[field, pl.ds(0, sx, stride=sy), :]
+            ys[field, 1] = fbuf[field, pl.ds(sy - 1, sx, stride=sy), :]
 
     def send(field, ks):
         for k in ks:
@@ -331,13 +351,11 @@
                 entry = float(derivative[a, face])
                 if inner is None or entry == 0.0:
                     continue
-                term = entry * geo_ref[0, pl.ds((base + a) * sy, sy), :] * inner
+                term = entry * fbuf[GEO_X, pl.ds((base + a) * sy, sy), :] * inner
                 total = term if total is None else total + term
             planes.append(total)
-        both = sum_yz(jnp.concatenate(planes, axis=0))
-        xs[field, 0] = both[:sy]
-        xs[field, 1] = both[sy:]
-        send(field, X_DIRS)
+        xs[field, 0], xs[field, 1] = planes
+        send(field, X_ONLY)
 
     def table_copy(k):
         o = OPPOSITE[k]
@@ -375,23 +393,18 @@
             + mass[...] * value
         )
 
-    def with_neighbours(value):
-        return element_operator(value, gm.at[0], gm.at[1], gm.at[2])
-
     loaded("hel", "res")
-    prepare(RES, res_ref[...], True)
+    prepare(RES, sum_x(sum_y(sum_z(res_ref[...]))))
     loaded("geo", "sqz", "sqy")
     square = derivative * derivative
-    diagonal_x = along_x(geo_ref[0], square.T)
-    for side, first in ((0, 0), (1, rows - sy)):
-        tsend[side, 0] = geo_ref[1, pl.ds(first, sy), :]
-        tsend[side, 1] = geo_ref[2, pl.ds(first, sy), :]
-        tsend[side, 2] = diagonal_x[first : first + sy] + hel_ref[pl.ds(first, sy), :]
-    prepare(
-        DIAG,
-        diagonal_x + left(sqy_ref, geo_ref[1]) + right(geo_ref[2], sqz_ref) + hel_ref[...],
-        True,
+    diagonal = (
+        along_x(geo_ref[0], square.T)
+        + left(sqy_ref, geo_ref[1])
+        + right(geo_ref[2], sqz_ref)
+        + hel_ref[...]
     )
+    prepare(DIAG, sum_x(sum_y(sum_z(diagonal))))
+    prepare(GEO_X, sum_y(sum_z(geo_ref[0])))
     csend[...] = cc_ref[...]
     lanes = lax.broadcasted_iota(jnp.int32, (1, padded), 1)
     values = []
@@ -422,15 +435,16 @@
 
     for j in range(1, nn):
         coarse_copy(csend, crecv.at[j], csend_sem, crecv_sem, j).start()
-    send(DIAG, Y_DIRS)
-    send(RES, Y_DIRS)
-    send(DIAG, X_DIRS)
-    send(RES, X_DIRS)
-    for k in (0, 1):
-
-        @pl.when(exists(DIRS[k]))
-        def _():
-            table_copy(k).start()
+    for field in (DIAG, RES, GEO_X):
+        send(field, Y_DIRS)
+    for field in (DIAG, RES):
+        send(field, X_DIRS)
+    prepare(GEO_Y, sum_x(sum_z(geo_ref[1])))
+    prepare(GEO_Z, sum_x(sum_y(geo_ref[2])))
+    prepare(MASS, sum_x(sum_y(sum_z(hel_ref[...]))))
+    send(GEO_Y, X_ONLY)
+    for field in (GEO_Z, MASS):
+        send(field, (*X_DIRS, *Y_DIRS))
 
     theta = 0.5 * (high_bound + low_bound)
     delta = 0.5 * (high_bound - low_bound)
@@ -438,49 +452,36 @@
 
     finish(DIAG, Y_DIRS)
     finish(RES, Y_DIRS)
+    finish(GEO_X, Y_DIRS)
     inverse = 1.0 / fbuf[DIAG]
     residual = fbuf[RES]
     update = inverse * residual * (1.0 / theta)
     inner_terms(FIRST, update)
-
-    loaded("pz", "pxy", "dz", "dy", "dzt", "dyt", "pxyt")
-    pieces = [csend[...]]
-    for j in range(1, nn):
-        coarse_copy(csend, crecv.at[j], csend_sem, crecv_sem, j).wait_recv()
-        pieces.append(crecv[j])
-    whole = jnp.concatenate(pieces, axis=1)
-    contract_last = (((1,), (1,)), ((), ()))
-    picked = jnp.sum(
-        lax.dot_general(
-            three_rows(whole), onehot[...], contract_last, preferred_element_type=jnp.float32
-        ),
-        axis=0,
-        keepdims=True,
-    )
-    columns = pairs * 8 * ez
-    groups = pairs * 4
-    row_of = lax.broadcasted_iota(jnp.int32, (groups, columns), 1) // (2 * ez)
-    mine = row_of == lax.broadcasted_iota(jnp.int32, (groups, columns), 0)
-    spread = jnp.where(mine, picked, 0.0)
-    along_z = jnp.dot(
-        spread, pz_ref[...], precision=HIGHEST, preferred_element_type=jnp.float32
-    )
-    correction = jnp.dot(
-        pxy_ref[...], along_z, precision=HIGHEST, preferred_element_type=jnp.float32
-    )
-    prepare(CORR, element_operator(correction, geo_ref.at[1], geo_ref.at[2], hel_ref), True)
-    send(CORR, (*Y_DIRS, *X_DIRS))
-
-    gm[0] = geo_ref[1]
-    gm[1] = geo_ref[2]
-    gm[2] = hel_ref[...]
+    for side, base, face in ((0, 0, 0), (1, sx - NODES, NODES - 1)):
+        total = None
+        for a in range(NODES):
+            entry = float(derivative[a, face]) ** 2
+            term = entry * fbuf[GEO_X, pl.ds((base + a) * sy, sy), :]
+            total = term if total is None else total + term
+        tsend[side, 0] = total
+    for k in (0, 1):
+
+        @pl.when(exists(DIRS[k]))
+        def _():
+            table_copy(k).start()
+
+
+    loaded(*ORDER[ORDER.index("ids") + 1 :])
+
+    finish(GEO_Y, X_ONLY)
+    for field in (GEO_Z, MASS):
+        finish(field, (*Y_DIRS, *X_DIRS))
     for k, first in ((0, 0), (1, rows - sy)):
 
         @pl.when(exists(DIRS[k]))
         def _():
             table_copy(OPPOSITE[k]).wait_recv()
-            for part in range(3):
-                gm[part, pl.ds(first, sy), :] += trecv[k, part]
+            fbuf[MASS, pl.ds(first, sy), :] += trecv[k, 0]
 
     finish(DIAG, X_DIRS)
     finish(RES, X_DIRS)
@@ -491,13 +492,18 @@
     update = patch(update, inverse_faces * residual_faces * (1.0 / theta))
 
     rho = 1.0 / sigma
-    solution_value = correction
+    solution_value = jnp.zeros((rows, sz), jnp.float32)
     count = 2 * DEGREE - 1
     for number in range(count):
         solution_value = solution_value + update
         field = FIRST + number
-        prepare(field, with_neighbours(update), False)
+        prepare(field, left(sdyt_ref, left(dy_ref, update) * fbuf[GEO_Y]))
         send(field, Y_DIRS)
+        fbuf[field] += (
+            sum_x(along_x(along_x(update, derivative) * fbuf[GEO_X], derivative.T))
+            + right(right(update, dz_ref) * fbuf[GEO_Z], sdzt_ref)
+            + fbuf[MASS] * update
+        )
         if number == DEGREE - 1:
             finish(CORR, (*Y_DIRS, *X_DIRS))
         finish(field, Y_DIRS)
@@ -515,6 +521,34 @@
             update = keep * old_update + gain * inverse * residual
         if number + 1 < count:
             inner_terms(field + 1, update)
+        if number == 0:
+            pieces = [csend[...]]
+            for j in range(1, nn):
+                coarse_copy(csend, crecv.at[j], csend_sem, crecv_sem, j).wait_recv()
+                pieces.append(crecv[j])
+            whole = jnp.concatenate(pieces, axis=1)
+            contract_last = (((1,), (1,)), ((), ()))
+            picked = jnp.sum(
+                lax.dot_general(
+                    three_rows(whole), onehot[...], contract_last, preferred_element_type=jnp.float32
+                ),
+                axis=0,
+                keepdims=True,
+            )
+            columns = pairs * 8 * ez
+            groups = pairs * 4
+            row_of = lax.broadcasted_iota(jnp.int32, (groups, columns), 1) // (2 * ez)
+            mine = row_of == lax.broadcasted_iota(jnp.int32, (groups, columns), 0)
+            spread = jnp.where(mine, picked, 0.0)
+            along_z = jnp.dot(
+                spread, pz_ref[...], precision=HIGHEST, preferred_element_type=jnp.float32
+            )
+            correction = jnp.dot(
+                pxy_ref[...], along_z, precision=HIGHEST, preferred_element_type=jnp.float32
+            )
+            product = element_operator(correction, geo_ref.at[1], geo_ref.at[2], hel_ref)
+            prepare(CORR, sum_x(sum_y(sum_z(product))))
+            send(CORR, (*Y_DIRS, *X_DIRS))
         if number == DEGREE:
             point = lax.broadcasted_iota(jnp.int32, (rows, sz), 0)
             x, y = point // sy, point % sy
@@ -548,7 +582,7 @@
                 psend[j] = partial[:, at : at + padded]
                 coarse_copy(psend.at[j], precv.at[j], psend_sem, precv_sem, j).start()
             own = partial[:, :padded]
-        finish(field, X_DIRS)
+        finish(field, X_ONLY)
         residual_faces = faces_of(old_residual) - face_part(field)
         residual = patch(residual, residual_faces)
         if number == DEGREE - 1:
@@ -561,7 +595,7 @@
             update = patch(
                 update, keep * faces_of(old_update) + gain * inverse_faces * residual_faces
             )
-    solution_value = solution_value + update
+    solution_value = correction + solution_value + update
     out_ref[...] = solution_value
 
     for j in range(1, nn):
@@ -573,9 +607,9 @@
         coarse_copy(csend, crecv.at[j], csend_sem, crecv_sem, j).wait_send()
         coarse_copy(psend.at[j], precv.at[j], psend_sem, precv_sem, j).wait_send()
     for field in range(FIELDS):
-        for k, step in enumerate(DIRS):
-
-            @pl.when(exists(step))
+        for k in directions(field):
+
+            @pl.when(exists(DIRS[k]))
             def _():
                 descriptor(field, k).wait_send()
 
@@ -613,6 +647,8 @@
         "dz": right_table(np.kron(eye_z, derivative.T)),
         "dzt": right_table(np.kron(eye_z, derivative)),
         "sqz": right_table(np.kron(eye_z, square)),
+        "sdyt": left_table(np.kron(np.eye(sx), chain(sy)) @ np.kron(eye_y, derivative.T)),
+        "sdzt": right_table(np.kron(eye_z, derivative) @ chain(sz)),
         "pxy": pxy,
         "pxyt": np.ascontiguousarray(pxy.T),
         "pz": pz,
@@ -642,9 +678,8 @@
             pltpu.VMEM((FIELDS, 2, sy, sz), f32),
             pltpu.VMEM((FIELDS, 2, sx, sz), f32),
             pltpu.VMEM((FIELDS, 4, 1, sz), f32),
-            pltpu.VMEM((3, rows, sz), f32),
-            pltpu.VMEM((2, 3, sy, sz), f32),
-            pltpu.VMEM((2, 3, sy, sz), f32),
+            pltpu.VMEM((2, 1, sy, sz), f32),
+            pltpu.VMEM((2, 1, sy, sz), f32),
             pltpu.VMEM((pairs * 8 * ez, nn * padded), jnp.bfloat16),
             pltpu.VMEM((1, padded), f32),
             pltpu.VMEM((nn, 1, padded), f32),

time: 22.8 us -> 24.2 us (1.061)
  Pallas kernels: 20.9 us -> 22.2 us
    pallas_call x1, Pallas kernels: 20.9 us -> 22.2 us  [on_device(): pl.pallas_call(functools.partial(kernel, (nw, nn, sx, sy, sz, slots, padd...]
where the time goes in v4:
time: 24.2 us; the launch traced here: 24.1 us
  Pallas kernels  22.2 us (92%)
  local copies, waits for them, and re-layouts  1.17 us (5%)
  between operations  0.64 us (3%)
    pallas_call x1, Pallas kernels, on_device(): pl.pallas_call(functools.partial(kernel, (nw, nn, sx, sy, sz, slots, padd...  22.2 us
    unnamed x2, local copies, waits for them, and re-layouts  1.17 us

profile of v4, /device:TPU:0, one launch (start us, length us, event | category | flops | bytes accessed | tf_op | source)
XLA Modules:
  0.0 24.1 jit_solution(10851982236673369760)
XLA Ops:
  0.6 22.2 %shard_map.167 = (f32[256,128]{1,0:T(8,128)S(1)}, f32[1,128]{1,0:T(1,128)S(1)}) custom-call(f32[1,128]{1,0:T(1,128)} %bitcast.15, f32[256,128]{1,0:T(8,128)} %bitcast.12, f32[256,128]{1,0:T(8,128)} %bitcast.13, f32[3,256,128]{2,1,0:T(8,128)} %bitcast.11, bf16[256,256]{1,0:T(8,128)(2,1)} %constant.22.clone.refs_3_, ...), custom_call_target="tpu_custom_call" | custom-call | tf_op jit(solution)/shard_map/pallas_call | solution.py:664
  22.9 0.7 %copy.20 = f32[16,16,128]{2,1,0:T(8,128)} copy(f32[16,16,128]{2,1,0:T(8,128)S(1)} %bitcast.9) | data formatting | bytes 262144
  23.5 0.5 %copy.21 = f32[128]{0:T(128)} copy(f32[128]{0:T(128)S(1)} %bitcast.10) | data formatting | bytes 1024
